TPU v7x, 128 devices: a whole 4x4x4 slice. The times are simulated.
128 devices in a mesh: dp: 4 (over y), band: 32 (over x, z, core).
Axes of the slice: x: 4, y: 4, z: 4, core: 2. Of those that a mesh axis runs over, the one named last changes fastest.
Arguments:
- features: bfloat16 [4, 256, 5504], P('dp', None, 'band'), may hold values from -6 to 6
- corner_rows: int32 [4, 8, 64, 5504], P('dp', None, None, 'band'), may hold values from 0 to 5503, as said below
- corner_weights: float32 [4, 8, 64, 5504], P('dp', None, None, 'band'), may hold values from 0 to 1, as said below
- out_grad: bfloat16 [4, 256, 5504], P('dp', None, 'band'), may hold values from -6 to 6
- value_weight: bfloat16 [256, 256], replicated, may hold values from -0.375 to 0.375
- logit_weight: bfloat16 [256, 128], replicated, may hold values from -0.375 to 0.375
- output_weight: bfloat16 [256, 256], replicated, may hold values from -0.375 to 0.375
Outputs:
- input_grad: bfloat16 [4, 256, 5504], P('dp', None, 'band')
- value_weight_grad: float32 [256, 256], replicated
- logit_weight_grad: float32 [256, 128], replicated
- output_weight_grad: float32 [256, 256], replicated
Inputs may be any that keep to these rules, and one draw needn't show every extreme that they name: `corner_rows`: cells are numbered band by band: cell t belongs to band t // 172; in a band's block the first 128 cells are of level 0, then 128 // 4 of level 1, 8 of level 2, 4 of level 3. An entry with k // 16 = l names a cell of level l. Every entry of a query in band b names a cell of band b - 1, b or b + 1. `corner_weights`: each group of four corners holds (1 - a)(1 - b), (1 - a) b, a (1 - b), a b for some a and b in [0, 1), so the four sum to one.
All inputs are finite; a program needn't handle non-finite values.
Results may differ from a plain program's by a relative error of at most 0.0064.
Values may be sent and summed in bfloat16 or wider, within the bound.
A program may use at most 64 MiB of HBM per device.

v0:
```python
import jax
import jax.numpy as jnp
from jax import lax
from jax.sharding import PartitionSpec as P

HEADS = 8
LEVELS = 4
POINTS = 4


def padded(block, sides, width):
    for axis, dim in sides:
        count = lax.axis_size(axis)
        forward = [(i, i + 1) for i in range(count - 1)]
        backward = [(target, source) for source, target in forward]
        low = lax.ppermute(
            lax.slice_in_dim(block, block.shape[dim] - width, None, axis=dim), axis, forward
        )
        high = lax.ppermute(lax.slice_in_dim(block, 0, width, axis=dim), axis, backward)
        block = jnp.concatenate([low, block, high], axis=dim)
    return block


def packed_total(arrays, axis):
    flat, at, outs = (jnp.concatenate([a.reshape(-1) for a in arrays]), 0, [])
    running = lax.psum(flat, axis)
    for a in arrays:
        outs.append(running[at : at + a.size].reshape(a.shape))
        at += a.size
    return tuple(outs)


def contract(left, right):
    return lax.dot_general(
        left, right, (((1,), (1,)), ((), ())), preferred_element_type=jnp.float32
    )


def head_pass(inputs):
    lookup_head, rows_head, blend_head, bilinear, grad_head = inputs
    picked = jnp.take(lookup_head, rows_head, axis=1)
    sampled = jnp.einsum("ekq,kq->eq", picked, blend_head, preferred_element_type=jnp.float32)
    blend_grad = jnp.einsum("ekq,eq->kq", picked, grad_head, preferred_element_type=jnp.float32)
    attn_grad = jnp.sum((blend_grad * bilinear).reshape(-1, 4, bilinear.shape[1]), axis=1)
    return (sampled, attn_grad)


def spread(rows_head, blend_head, grad_head, extent):
    contribution = (
        blend_head.astype(jnp.float32)[None, :, :] * grad_head.astype(jnp.float32)[:, None, :]
    )
    partial_value = jnp.zeros((grad_head.shape[0], extent), jnp.float32)
    return partial_value.at[:, rows_head].add(contribution, mode="drop")


def body(
    features, corner_rows, corner_weights, out_grad, value_weight, logit_weight, output_weight
):
    inputs = features[0]
    cotangent = out_grad[0]
    band_cells = inputs.shape[1]
    head_count = HEADS
    head_size = inputs.shape[0] // head_count
    points_all = LEVELS * POINTS
    values_map = jnp.dot(value_weight.T, inputs, preferred_element_type=jnp.float32).astype(
        jnp.bfloat16
    )
    logits = jnp.dot(logit_weight.T, inputs, preferred_element_type=jnp.float32).reshape(
        head_count, points_all, -1
    )
    exponent = jnp.exp(logits)
    attention = exponent / jnp.sum(exponent, axis=1, keepdims=True)
    blend = (jnp.repeat(attention, 4, axis=1) * corner_weights[0]).astype(jnp.bfloat16)
    sample_grad = jnp.dot(output_weight, cotangent, preferred_element_type=jnp.float32).astype(
        jnp.bfloat16
    )
    lookup = padded(values_map, (("band", 1),), band_cells)
    global_rows = corner_rows[0]
    my_band = lax.axis_index("band")
    local_rows = (global_rows // band_cells - my_band + 1) * band_cells + global_rows % band_cells
    grad_heads = sample_grad.reshape(head_count, head_size, -1)
    sampled, attn_grad = lax.map(
        head_pass,
        (
            lookup.reshape(head_count, head_size, -1),
            local_rows,
            blend,
            corner_weights[0],
            grad_heads,
        ),
    )
    sampled = sampled.reshape(head_count * head_size, -1).astype(jnp.bfloat16)
    partial_value = lax.map(
        lambda item: spread(item[0], item[1], item[2], 3 * band_cells),
        (local_rows, blend, grad_heads),
    )
    partial_value = partial_value.reshape(head_count * head_size, -1)
    beside_all = padded(partial_value, (("band", 1),), band_cells)
    summed = (
        beside_all[:, :band_cells]
        + beside_all[:, 2 * band_cells : 3 * band_cells]
        + beside_all[:, 4 * band_cells :]
    )
    value_grad = summed.astype(jnp.bfloat16)
    logit_grad = attention * (attn_grad - jnp.sum(attention * attn_grad, axis=1, keepdims=True))
    logit_grad = logit_grad.reshape(head_count * points_all, -1).astype(jnp.bfloat16)
    input_grad = jnp.dot(value_weight, value_grad, preferred_element_type=jnp.float32) + jnp.dot(
        logit_weight, logit_grad, preferred_element_type=jnp.float32
    )
    grad_value_w, grad_logit_w, grad_output_w = packed_total(
        (contract(inputs, value_grad), contract(inputs, logit_grad), contract(sampled, cotangent)),
        ("dp", "band"),
    )
    norm_scale = 1.0 / float(lax.axis_size("dp") * lax.axis_size("band") * band_cells) ** 0.5
    return (
        input_grad.astype(jnp.bfloat16)[None],
        grad_value_w * norm_scale,
        grad_logit_w * norm_scale,
        grad_output_w * norm_scale,
    )


def solution(mesh):
    placed = (
        P("dp", None, "band"),
        P("dp", None, None, "band"),
        P("dp", None, None, "band"),
        P("dp", None, "band"),
        P(),
        P(),
        P(),
    )
    return jax.shard_map(
        body,
        mesh=mesh,
        in_specs=placed,
        out_specs=(P("dp", None, "band"), P(), P(), P()),
        check_vma=False,
    )
```

profile of v0, /device:TPU:1, one launch (start us, length us, event | category | flops | bytes accessed | tf_op | source)
XLA Modules:
  0.0 1018.7 jit_solution(11657953802035154438)
XLA Ops:
  9.8 4.9 collective-permute-start.2
  21.4 557.9 %while.22 = (s32[]{:T(128)}, f32[8,32,516]{2,1,0:T(8,128)}, s32[8,64,172]{2,1,0:T(8,128)S(1)}, bf16[8,64,172]{2,1,0:T(8,128)(2,1)S(1)}, bf16[8,32,172]{2,1,0:T(8,128)(2,1)}, /*index=5*/s32[]{:T(128)}, f32[]{:T(128)}) while((s32[]{:T(128)}, f32[8,32,516]{2,1,0:T(8,128)}, s32[8,64,172]{2,1,0:T(8,128)S(1)}, bf16[8,64,172]{2,1,0:T(8,128)(2,1)S(1)}, ...), condition=%wide.region_3.4_spmd, body=%wide.region_1.3_spmd.sunk | while | flops 754050 | bytes 7733593 | solution.py:93
  24.6 4.8 copy.51
  29.5 60.8 %scatter_custom_fusion.5 = f32[32,516]{0,1:T(8,128)S(1)} fusion(s32[11008]{0:T(1024)S(1)} %reshape.195, f32[11008,32]{1,0:T(8,128)} %copy.51, f32[]{:T(128)} %constant.39.clone.1..sunk), kind=kCustom, calls=%fused_computation.4.clone.1 | custom fusion | flops 352256 | bytes 66560 | tf_op jit(solution)/shard_map/while/body/eval_jaxpr/scatter-add | solution.py:53
  94.3 4.8 copy.51
  99.3 60.8 %scatter_custom_fusion.5 = f32[32,516]{0,1:T(8,128)S(1)} fusion(s32[11008]{0:T(1024)S(1)} %reshape.195, f32[11008,32]{1,0:T(8,128)} %copy.51, f32[]{:T(128)} %constant.39.clone.1..sunk), kind=kCustom, calls=%fused_computation.4.clone.1 | custom fusion | flops 352256 | bytes 66560 | tf_op jit(solution)/shard_map/while/body/eval_jaxpr/scatter-add | solution.py:53
  164.1 4.8 copy.51
  169.0 60.8 %scatter_custom_fusion.5 = f32[32,516]{0,1:T(8,128)S(1)} fusion(s32[11008]{0:T(1024)S(1)} %reshape.195, f32[11008,32]{1,0:T(8,128)} %copy.51, f32[]{:T(128)} %constant.39.clone.1..sunk), kind=kCustom, calls=%fused_computation.4.clone.1 | custom fusion | flops 352256 | bytes 66560 | tf_op jit(solution)/shard_map/while/body/eval_jaxpr/scatter-add | solution.py:53
  233.8 4.8 copy.51
  238.7 60.8 %scatter_custom_fusion.5 = f32[32,516]{0,1:T(8,128)S(1)} fusion(s32[11008]{0:T(1024)S(1)} %reshape.195, f32[11008,32]{1,0:T(8,128)} %copy.51, f32[]{:T(128)} %constant.39.clone.1..sunk), kind=kCustom, calls=%fused_computation.4.clone.1 | custom fusion | flops 352256 | bytes 66560 | tf_op jit(solution)/shard_map/while/body/eval_jaxpr/scatter-add | solution.py:53
  308.5 60.8 %scatter_custom_fusion.5 = f32[32,516]{0,1:T(8,128)S(1)} fusion(s32[11008]{0:T(1024)S(1)} %reshape.195, f32[11008,32]{1,0:T(8,128)} %copy.51, f32[]{:T(128)} %constant.39.clone.1..sunk), kind=kCustom, calls=%fused_computation.4.clone.1 | custom fusion | flops 352256 | bytes 66560 | tf_op jit(solution)/shard_map/while/body/eval_jaxpr/scatter-add | solution.py:53
  378.2 60.8 %scatter_custom_fusion.5 = f32[32,516]{0,1:T(8,128)S(1)} fusion(s32[11008]{0:T(1024)S(1)} %reshape.195, f32[11008,32]{1,0:T(8,128)} %copy.51, f32[]{:T(128)} %constant.39.clone.1..sunk), kind=kCustom, calls=%fused_computation.4.clone.1 | custom fusion | flops 352256 | bytes 66560 | tf_op jit(solution)/shard_map/while/body/eval_jaxpr/scatter-add | solution.py:53
  447.9 60.8 %scatter_custom_fusion.5 = f32[32,516]{0,1:T(8,128)S(1)} fusion(s32[11008]{0:T(1024)S(1)} %reshape.195, f32[11008,32]{1,0:T(8,128)} %copy.51, f32[]{:T(128)} %constant.39.clone.1..sunk), kind=kCustom, calls=%fused_computation.4.clone.1 | custom fusion | flops 352256 | bytes 66560 | tf_op jit(solution)/shard_map/while/body/eval_jaxpr/scatter-add | solution.py:53
  517.7 60.8 %scatter_custom_fusion.5 = f32[32,516]{0,1:T(8,128)S(1)} fusion(s32[11008]{0:T(1024)S(1)} %reshape.195, f32[11008,32]{1,0:T(8,128)} %copy.51, f32[]{:T(128)} %constant.39.clone.1..sunk), kind=kCustom, calls=%fused_computation.4.clone.1 | custom fusion | flops 352256 | bytes 66560 | tf_op jit(solution)/shard_map/while/body/eval_jaxpr/scatter-add | solution.py:53
  588.8 263.6 %while.23 = (s32[]{:T(128)}, bf16[8,32,172]{2,1,0:T(8,128)(2,1)}, f32[8,16,172]{2,1,0:T(8,128)}, bf16[8,64,172]{2,1,0:T(8,128)(2,1)S(1)}, s32[8,64,172]{2,1,0:T(...) while((s32[]{:T(128)}, bf16[8,32,172]{2,1,0:T(8,128)(2,1)}, ...), condition=%wide.region_6.7_spmd, body=%wide.region_4.6_spmd.sunk | while | flops 2947650 | bytes 9523897 | solution.py:82
  589.9 20.5 %gather_fusion = bf16[11008,32]{1,0:T(8,128)(2,1)S(1)} fusion(bf16[32,516]{0,1:T(8,128)(2,1)S(1)} %bitcast.154, s32[11264]{0:T(1024)S(1)} %pad_clamp_fusion.2), kind=kCustom, calls=%fused_computation.clone.1 | custom fusion | bytes 1453056 | tf_op jit(solution)/shard_map/while/body/eval_jaxpr/jit(_take)/gather | solution.py:41
  622.9 20.5 %gather_fusion = bf16[11008,32]{1,0:T(8,128)(2,1)S(1)} fusion(bf16[32,516]{0,1:T(8,128)(2,1)S(1)} %bitcast.154, s32[11264]{0:T(1024)S(1)} %pad_clamp_fusion.2), kind=kCustom, calls=%fused_computation.clone.1 | custom fusion | bytes 1453056 | tf_op jit(solution)/shard_map/while/body/eval_jaxpr/jit(_take)/gather | solution.py:41
  655.8 20.5 %gather_fusion = bf16[11008,32]{1,0:T(8,128)(2,1)S(1)} fusion(bf16[32,516]{0,1:T(8,128)(2,1)S(1)} %bitcast.154, s32[11264]{0:T(1024)S(1)} %pad_clamp_fusion.2), kind=kCustom, calls=%fused_computation.clone.1 | custom fusion | bytes 1453056 | tf_op jit(solution)/shard_map/while/body/eval_jaxpr/jit(_take)/gather | solution.py:41
  688.8 20.5 %gather_fusion = bf16[11008,32]{1,0:T(8,128)(2,1)S(1)} fusion(bf16[32,516]{0,1:T(8,128)(2,1)S(1)} %bitcast.154, s32[11264]{0:T(1024)S(1)} %pad_clamp_fusion.2), kind=kCustom, calls=%fused_computation.clone.1 | custom fusion | bytes 1453056 | tf_op jit(solution)/shard_map/while/body/eval_jaxpr/jit(_take)/gather | solution.py:41
  721.7 20.5 %gather_fusion = bf16[11008,32]{1,0:T(8,128)(2,1)S(1)} fusion(bf16[32,516]{0,1:T(8,128)(2,1)S(1)} %bitcast.154, s32[11264]{0:T(1024)S(1)} %pad_clamp_fusion.2), kind=kCustom, calls=%fused_computation.clone.1 | custom fusion | bytes 1453056 | tf_op jit(solution)/shard_map/while/body/eval_jaxpr/jit(_take)/gather | solution.py:41
  754.7 20.5 %gather_fusion = bf16[11008,32]{1,0:T(8,128)(2,1)S(1)} fusion(bf16[32,516]{0,1:T(8,128)(2,1)S(1)} %bitcast.154, s32[11264]{0:T(1024)S(1)} %pad_clamp_fusion.2), kind=kCustom, calls=%fused_computation.clone.1 | custom fusion | bytes 1453056 | tf_op jit(solution)/shard_map/while/body/eval_jaxpr/jit(_take)/gather | solution.py:41
  787.6 20.5 %gather_fusion = bf16[11008,32]{1,0:T(8,128)(2,1)S(1)} fusion(bf16[32,516]{0,1:T(8,128)(2,1)S(1)} %bitcast.154, s32[11264]{0:T(1024)S(1)} %pad_clamp_fusion.2), kind=kCustom, calls=%fused_computation.clone.1 | custom fusion | bytes 1453056 | tf_op jit(solution)/shard_map/while/body/eval_jaxpr/jit(_take)/gather | solution.py:41
  820.6 20.5 %gather_fusion = bf16[11008,32]{1,0:T(8,128)(2,1)S(1)} fusion(bf16[32,516]{0,1:T(8,128)(2,1)S(1)} %bitcast.154, s32[11264]{0:T(1024)S(1)} %pad_clamp_fusion.2), kind=kCustom, calls=%fused_computation.clone.1 | custom fusion | bytes 1453056 | tf_op jit(solution)/shard_map/while/body/eval_jaxpr/jit(_take)/gather | solution.py:41
  858.9 148.8 %all-reduce.2.cloned.1.call-done = f32[163840]{0:T(1024)} async-done(((f32[163840]{0:T(1024)}), f32[163840]{0:T(1024)}) %all-reduce.2.cloned.1.call-update) | async-done | bytes 655376 | tf_op jit(solution)/shard_map/psum | solution.py:26
  (293 shorter events, 180.1 us)
Async XLA Ops:
  7.2 12.6 %copy-start.7 = (bf16[1,256,172]{1,2,0:T(8,128)(2,1)S(1)}, bf16[1,256,172]{1,2,0:T(8,128)(2,1)}, u32[]{:S(2)}) copy-start(bf16[1,256,172]{1,2,0:T(8,128)(2,1)} %param.14) | copy-start | bytes 264196
  7.2 12.6 %copy-start.9 = (bf16[256,256]{1,0:T(8,128)(2,1)S(1)}, bf16[256,256]{1,0:T(8,128)(2,1)}, u32[]{:S(2)}) copy-start(bf16[256,256]{1,0:T(8,128)(2,1)} %param.17) | copy-start | bytes 393220
  7.2 13.5 %copy-start.4 = (f32[1,8,64,172]{3,2,1,0:T(8,128)S(1)}, f32[1,8,64,172]{3,2,1,0:T(8,128)}, u32[]{:S(2)}) copy-start(f32[1,8,64,172]{3,2,1,0:T(8,128)} %param.13) | copy-start | bytes 1056772
  7.2 1000.5 %all-reduce.2.cloned.1.call-start = ((), (), s32[]{:S(2)}) async-start(), calls=%async_computation | async-start | bytes 1310720 | tf_op jit(solution)/shard_map/psum | solution.py:26
  9.8 577.0 %collective-permute-start.2 = (bf16[256,172]{0,1:T(8,128)(2,1)}, bf16[256,172]{0,1:T(8,128)(2,1)}, u32[]{:S(2)}, u32[]{:S(2)}) collective-permute-start(bf16[256,172]{0,1:T(8,128)(2,1)} %convolution_convert_fusion), channel_id=1, source_target_pairs={{0,1},{1,2},{2,3},{3,4},{4,5},{5,6},{6,7},{7,8},{8,9},{9,10},{10,1... | collective-permute-start | bytes 264200 | tf_op jit(solution)/shard_map/ppermute | solution.py:16
  14.7 572.1 %collective-permute-start.3 = (bf16[256,172]{0,1:T(8,128)(2,1)}, bf16[256,172]{0,1:T(8,128)(2,1)}, u32[]{:S(2)}, u32[]{:S(2)}) collective-permute-start(bf16[256,172]{0,1:T(8,128)(2,1)} %convolution_convert_fusion), channel_id=1, source_target_pairs={{1,0},{2,1},{3,2},{4,3},{5,4},{6,5},{7,6},{8,7},{9,8},{10,9},{11,1... | collective-permute-start | bytes 264200 | tf_op jit(solution)/shard_map/ppermute | solution.py:19
  16.6 4.2 copy-start.6
  581.2 273.9 %collective-permute-start = (f32[256,172]{1,0:T(8,128)}, f32[256,172]{1,0:T(8,128)}, u32[]{:S(2)}, u32[]{:S(2)}) collective-permute-start(f32[256,172]{1,0:T(8,128)} %get-tuple-element.126), channel_id=1, source_target_pairs={{0,1},{1,2},{2,3},{3,4},{4,5},{5,6},{6,7},{7,8},{8,9},{9,10},{10,1... | collective-permute-start | bytes 528392 | tf_op jit(solution)/shard_map/ppermute | solution.py:16
  584.9 270.2 %collective-permute-start.1 = (f32[256,172]{1,0:T(8,128)}, f32[256,172]{1,0:T(8,128)}, u32[]{:S(2)}, u32[]{:S(2)}) collective-permute-start(f32[256,172]{1,0:T(8,128)} %get-tuple-element.127), channel_id=1, source_target_pairs={{1,0},{2,1},{3,2},{4,3},{5,4},{6,5},{7,6},{8,7},{9,8},{10,9},{11,1... | collective-permute-start | bytes 528392 | tf_op jit(solution)/shard_map/ppermute | solution.py:19
  588.8 264.8 %copy-start.3 = (bf16[1,256,172]{1,2,0:T(8,128)(2,1)S(1)}, bf16[1,256,172]{1,2,0:T(8,128)(2,1)}, u32[]{:S(2)}) copy-start(bf16[1,256,172]{1,2,0:T(8,128)(2,1)} %param.11) | copy-start | bytes 264196
  588.8 1.1 copy-start.1
  613.0 8.7 copy-start.2
  621.7 1.1 copy-start.1
  646.0 8.7 copy-start.2
  654.7 1.1 copy-start.1
  678.9 8.7 copy-start.2
  687.6 1.1 copy-start.1
  711.9 8.7 copy-start.2
  720.6 1.1 copy-start.1
  744.8 8.7 copy-start.2
  777.8 8.7 copy-start.2
  810.7 8.7 copy-start.2
  843.7 8.7 copy-start.2
  855.1 2.7 copy-start.8
  (5 other events, 4.9 us)
Sparse Core Ops, SparseCore 0:
  857.9 149.7 all-reduce.1
where the time goes:
time: 1020 us
  other arithmetic  528 us (52%)
  local copies, waits for them, and re-layouts  309 us (30%)
  waiting for transfers between devices  149 us (15%)
  between operations  14.3 us (1%)
  starting transfers between devices  12.4 us (1%)
    scatter-add x8, other arithmetic, spread(): return partial_value.at[:, rows_head].add(contribution, mode='drop')  487 us
    gather x24, local copies, waits for them, and re-layouts, head_pass(): picked = jnp.take(lookup_head, rows_head, axis=1)  219 us
    psum x1, waiting for transfers between devices, packed_total(): running = lax.psum(flat, axis)  149 us
    mul x16, local copies, waits for them, and re-layouts, spread(): blend_head.astype(jnp.float32)[None, :, :]  56 us
  transfers between devices with their start and end apart: 5, of which 1 were waited for; matrix products, arithmetic and copies ran while one was open for 82% of the time, Pallas kernels for 0%

commit v1 on v0

v1 whole, which is shorter than its diff:
```python
import functools

import jax
import jax.numpy as jnp
from jax import lax
from jax.experimental import pallas as pl
from jax.experimental.pallas import tpu as pltpu
from jax.sharding import PartitionSpec as P

HEADS = 8
LEVELS = 4
POINTS = 4
D = 256
CELLS = 172
PAD = 176
TAIL = CELLS - 128
GAP = 128 - 2 * TAIL
LANES = 384
HEAD = D // HEADS
PTS = LEVELS * POINTS
BF = jnp.bfloat16
F32 = jnp.float32


def dot(a, b, ca=1, cb=0):
    return lax.dot_general(a, b, (((ca,), (cb,)), ((), ())), preferred_element_type=F32)


def local_kernel(
    x_ref,
    rows_ref,
    cw_ref,
    og_ref,
    vw_ref,
    lw_ref,
    ow_ref,
    low_ref,
    own_ref,
    high_ref,
    lg_ref,
    gv_ref,
    gl_ref,
    go_ref,
    v_s,
    att_s,
    g_s,
    samp_s,
    rep_s,
    vg_s,
    wide_s,
    m_s,
):
    band = lax.axis_index("band")
    x = x_ref[1]
    og = og_ref[...]
    for j in range(3):
        v_s[j] = dot(vw_ref[...], x_ref[j], 0, 0).astype(BF)
    logits = dot(lw_ref[...], x, 0, 0)
    att_s[...] = logits.reshape(HEADS, PTS, CELLS)
    g_s[...] = dot(ow_ref[...], og).astype(BF).astype(F32)

    def packed(first, second, rows):
        tail = jnp.concatenate(
            [first[:, 128:], second[:, 128:], jnp.zeros((rows, GAP), first.dtype)], axis=1
        )
        return [first[:, :128], second[:, :128], tail]

    def pair(i, carry):
        h0 = 2 * i
        h1 = 2 * i + 1
        hs = pl.ds(pl.multiple_of(i * 2 * HEAD, 2 * HEAD), 2 * HEAD)
        base = (band - 1) * CELLS
        cells = packed(rows_ref[h0] - base, rows_ref[h1] - base, 64)
        cw = packed(cw_ref[h0], cw_ref[h1], 64)
        logit = packed(att_s[h0], att_s[h1], PTS)
        g0 = g_s[pl.ds(pl.multiple_of(i * 2 * HEAD, HEAD), HEAD), :]
        g1 = g_s[pl.ds(pl.multiple_of(i * 2 * HEAD + HEAD, HEAD), HEAD), :]
        none = jnp.zeros((HEAD, 128), F32)
        gap = jnp.zeros((HEAD, 128 - TAIL), F32)
        top = [g0[:, :128], none, jnp.concatenate([g0[:, 128:], gap], axis=1)]
        bottom = [
            none,
            g1[:, :128],
            jnp.concatenate([none[:, :TAIL], g1[:, 128:], none[:, : 128 - 2 * TAIL]], axis=1),
        ]
        att = []
        for g in range(3):
            e = jnp.exp(logit[g])
            att.append(e / jnp.sum(e, axis=0, keepdims=True))
            for c in range(4):
                rep_s[pl.ds(c, PTS, stride=4), :] = att[g]
            over1 = cells[g] >= CELLS
            over2 = cells[g] >= 2 * CELLS
            r = cells[g] - jnp.where(over2, 2 * CELLS, jnp.where(over1, CELLS, 0))
            w = (rep_s[...] * cw[g]).astype(BF).astype(F32)
            zero = jnp.zeros_like(w)
            ls = slice(g * 128, (g + 1) * 128)
            wide_s[0, :, ls] = r.astype(F32)
            wide_s[1, :, ls] = jnp.where(over1, zero, w)
            wide_s[2, :, ls] = jnp.where(jnp.logical_and(over1, jnp.logical_not(over2)), w, zero)
            wide_s[3, :, ls] = jnp.where(over2, w, zero)

        def wide(n, k):
            row = jnp.broadcast_to(wide_s[n, pl.ds(k, 1), :], (16, LANES))
            return row.astype(BF)

        sub = lax.broadcasted_iota(jnp.int32, (16, LANES), 0)
        for cb in range(11):
            if cb < 8:
                levels = (0,)
            elif cb < 10:
                levels = (1,)
            else:
                levels = (2, 3)
            ids = (sub + cb * 16).astype(F32).astype(BF)
            acc = [jnp.zeros((16, LANES), BF) for _ in range(3)]
            for lev in levels:
                for k in range(lev * 16, lev * 16 + 16):
                    hit = wide(0, k) == ids
                    for j in range(3):
                        acc[j] = acc[j] + jnp.where(hit, wide(1 + j, k), jnp.zeros((), BF))
            for j in range(3):
                m_s[j, cb * 16 : cb * 16 + 16, :] = acc[j]

        gp = jnp.concatenate(
            [jnp.concatenate(top, axis=1), jnp.concatenate(bottom, axis=1)], axis=0
        ).astype(BF)
        samp = jnp.zeros((2 * HEAD, LANES), F32)
        for j in range(3):
            m_j = m_s[j, :CELLS, :]
            samp = samp + dot(v_s[j, hs, :], m_j)
            vg_s[j, hs, :] = dot(gp, m_j, 1, 1).astype(BF)
        s0 = jnp.concatenate([samp[:HEAD, :128], samp[:HEAD, 256 : 256 + TAIL]], axis=1)
        s1 = jnp.concatenate(
            [samp[HEAD:, 128:256], samp[HEAD:, 256 + TAIL : 256 + 2 * TAIL]], axis=1
        )
        samp_s[hs, :] = jnp.concatenate([s0, s1], axis=0).astype(BF)

        lgs = []
        for g in range(3):
            at = jnp.concatenate([cells[g], jnp.zeros((64, 128), jnp.int32)], axis=0).T
            over1 = at >= CELLS
            over2 = at >= 2 * CELLS
            r = at - jnp.where(over2, 2 * CELLS, jnp.where(over1, CELLS, 0))
            first = jnp.clip(r, 0, 127)
            rest = jnp.clip(r - 128, 0, 127)
            g_t = jnp.concatenate([top[g], bottom[g]], axis=0).T.astype(BF)
            pick = jnp.zeros((128, 128), F32)
            for j in range(3):
                score = dot(g_t, v_s[j, hs, :])
                tail = jnp.concatenate([score[:, 128:], jnp.zeros((128, 256 - CELLS), F32)], axis=1)
                a = jnp.take_along_axis(score[:, :128], first, axis=1, mode="promise_in_bounds")
                b = jnp.take_along_axis(tail, rest, axis=1, mode="promise_in_bounds")
                val = jnp.where(r < 128, a, b)
                if j == 0:
                    pick = val
                elif j == 1:
                    pick = jnp.where(over1, val, pick)
                else:
                    pick = jnp.where(over2, val, pick)
            rep_s[...] = pick.T[:64] * cw[g]
            ag = jnp.zeros((PTS, 128), F32)
            for c in range(4):
                ag = ag + rep_s[pl.ds(c, PTS, stride=4), :]
            lgs.append(att[g] * (ag - jnp.sum(att[g] * ag, axis=0, keepdims=True)))
        l0 = jnp.concatenate([lgs[0], lgs[2][:, :TAIL]], axis=1)
        l1 = jnp.concatenate([lgs[1], lgs[2][:, TAIL : 2 * TAIL]], axis=1)
        ks = pl.ds(pl.multiple_of(i * 2 * PTS, 2 * PTS), 2 * PTS)
        lg_ref[ks, :] = jnp.concatenate([l0, l1], axis=0).astype(BF)
        return carry

    lax.fori_loop(0, HEADS // 2, pair, 0)
    low_ref[...] = vg_s[0]
    own_ref[...] = vg_s[1]
    high_ref[...] = vg_s[2]
    gv = dot(x_ref[0], vg_s[0], 1, 1)
    gv = gv + dot(x, vg_s[1], 1, 1)
    gv = gv + dot(x_ref[2], vg_s[2], 1, 1)
    gv_ref[...] = gv
    gl_ref[...] = dot(x, lg_ref[...], 1, 1)
    go_ref[...] = dot(samp_s[...], og, 1, 1)


def local_pass(x3, rows, cw, og, vw, lw, ow):
    vm = pl.BlockSpec(memory_space=pltpu.VMEM)
    return pl.pallas_call(
        local_kernel,
        out_shape=(
            jax.ShapeDtypeStruct((D, CELLS), BF),
            jax.ShapeDtypeStruct((D, CELLS), BF),
            jax.ShapeDtypeStruct((D, CELLS), BF),
            jax.ShapeDtypeStruct((HEADS * PTS, CELLS), BF),
            jax.ShapeDtypeStruct((D, D), F32),
            jax.ShapeDtypeStruct((D, HEADS * PTS), F32),
            jax.ShapeDtypeStruct((D, D), F32),
        ),
        in_specs=[vm] * 7,
        out_specs=[vm] * 7,
        scratch_shapes=[
            pltpu.VMEM((3, D, CELLS), BF),
            pltpu.VMEM((HEADS, PTS, CELLS), F32),
            pltpu.VMEM((D, CELLS), F32),
            pltpu.VMEM((D, CELLS), BF),
            pltpu.VMEM((64, 128), F32),
            pltpu.VMEM((3, D, CELLS), BF),
            pltpu.VMEM((4, 64, LANES), F32),
            pltpu.VMEM((3, PAD, LANES), BF),
        ],
        name="local_pass",
    )(x3, rows, cw, og, vw, lw, ow)


def body(features, corner_rows, corner_weights, out_grad, vw, lw, ow):
    x = features[0]
    og = out_grad[0]
    count = lax.axis_size("band")
    up = [(i, (i + 1) % count) for i in range(count)]
    down = [(i, (i - 1) % count) for i in range(count)]
    below = lax.ppermute(x, "band", up)
    above = lax.ppermute(x, "band", down)
    x3 = jnp.stack([below, x, above])
    low, own, high, lg, gv, gl, go = local_pass(
        x3, corner_rows[0], corner_weights[0], og, vw, lw, ow
    )
    from_above = lax.ppermute(low, "band", down)
    from_below = lax.ppermute(high, "band", up)
    value_grad = (
        own.astype(F32) + from_above.astype(F32) + from_below.astype(F32)
    ).astype(BF)
    input_grad = dot(vw, value_grad) + dot(lw, lg)
    flat = jnp.concatenate([gv, gl, go], axis=1)
    total = lax.psum(flat, ("dp", "band"))
    scale = 1.0 / float(lax.axis_size("dp") * count * CELLS) ** 0.5
    total = total * scale
    return (
        input_grad.astype(BF)[None],
        total[:, :D],
        total[:, D : D + HEADS * PTS],
        total[:, D + HEADS * PTS :],
    )


def solution(mesh):
    placed = (
        P("dp", None, "band"),
        P("dp", None, None, "band"),
        P("dp", None, None, "band"),
        P("dp", None, "band"),
        P(),
        P(),
        P(),
    )
    return jax.shard_map(
        body,
        mesh=mesh,
        in_specs=placed,
        out_specs=(P("dp", None, "band"), P(), P(), P()),
        check_vma=False,
    )
```

time: 1020 us -> 196 us (0.19)
  other arithmetic: 528 us -> 3.96 us
  local copies, waits for them, and re-layouts: 309 us -> 4.84 us
  Pallas kernels: 0 us -> 12.7 us
    scatter-add x8 -> x0, other arithmetic: 487 us -> none  [spread(): return partial_value.at[:, rows_head].add(contribution, mode='drop')]
    gather x24 -> x0, local copies, waits for them, and re-layouts: 219 us -> none  [head_pass(): picked = jnp.take(lookup_head, rows_head, axis=1)]
    mul x18 -> x0, local copies, waits for them, and re-layouts: 57.5 us -> none  [the longest x16 56 us: spread(): blend_head.astype(jnp.float32)[None, :, :]]
    dynamic_update_slice x32 -> x0, local copies, waits for them, and re-layouts: 15.9 us -> none  [the longest x16 9.68 us: body(): lax.map(head_pass, (lookup.reshape(head_count, head_size, -1), local_rows...]
    pallas_call x0 -> x1, Pallas kernels: none -> 12.7 us  [local_pass(): pl.pallas_call(local_kernel, out_shape=(jax.ShapeDtypeStruct((D, CELLS),...]
    mul x26 -> x1, other arithmetic: 11.4 us -> 1.14 us  [body(): total = total * scale]
  transfers between devices with their start and end apart: 5 -> 5, of which waited for: 1 -> 3; matrix products, arithmetic and copies ran while one was open for 82% -> 2% of each run, Pallas kernels for 0% -> 0%
where the time goes in v1:
time: 196 us
  waiting for transfers between devices  149 us (76%)
  between operations  14.1 us (7%)
  Pallas kernels  12.7 us (6%)
  starting transfers between devices  10.1 us (5%)
  local copies, waits for them, and re-layouts  4.84 us (2%)
  other arithmetic  3.96 us (2%)
    psum x1, waiting for transfers between devices, body(): total = lax.psum(flat, ('dp', 'band'))  145 us
    pallas_call x1, Pallas kernels, local_pass(): pl.pallas_call(local_kernel, out_shape=(jax.ShapeDtypeStruct((D, CELLS),...  12.7 us
    ppermute x1, starting transfers between devices, body(): from_above = lax.ppermute(low, 'band', down)  6.87 us
  transfers between devices with their start and end apart: 5, of which 3 were waited for; matrix products, arithmetic and copies ran while one was open for 2% of the time, Pallas kernels for 0%

profile of v1, /device:TPU:1, one launch (start us, length us, event | category | flops | bytes accessed | tf_op | source)
XLA Modules:
  0.0 195.7 jit_solution(13829992433428781197)
XLA Ops:
  7.2 0.0 all-reduce.2.cloned.1.call-start
  7.2 1.0 copy.11
  8.2 1.5 collective-permute-start.1
  9.7 1.7 collective-permute-start
  11.4 0.8 copy.13
  12.1 1.8 collective-permute-done.1
  14.0 2.3 %collective-permute-done = bf16[256,172]{1,0:T(8,128)(2,1)S(1)} collective-permute-done((bf16[256,172]{1,0:T(8,128)(2,1)S(1)}, bf16[256,172]{1,0:T(8,128)(2,1)S(1)}, u32[]{:S(2)}, u32[]{:S(2)}) %collective-permute-start) | collective-permute-done | bytes 88096 | tf_op jit(solution)/shard_map/ppermute | solution.py:219
  16.3 0.8 pad_maximum_fusion.1.x_ref
  17.1 12.7 %local_pass.1 = (bf16[256,172]{1,0:T(8,128)(2,1)}, bf16[256,172]{1,0:T(8,128)(2,1)}, bf16[256,172]{1,0:T(8,128)(2,1)}, bf16[128,172]{1,0:T(8,128)(2,1)}, f32[256...) custom-call(bf16[3,256,172]{2,1,0:T(8,128)(2,1)} %pad_maximum_fusion.1.x_ref, s32[8,64,172]{2,1,0:T(8,128)} %bitcast.15, ...), custom_call_target="tpu_custom_call" | custom-call | tf_op jit(solution)/shard_map/local_pass/pallas_call | solution.py:186
  29.9 6.9 %collective-permute-start.2 = (bf16[256,172]{1,0:T(8,128)(2,1)}, bf16[256,172]{1,0:T(8,128)(2,1)S(1)}, u32[]{:S(2)}, u32[]{:S(2)}) collective-permute-start(bf16[256,172]{1,0:T(8,128)(2,1)} %get-tuple-element.12), channel_id=1, source_target_pairs={{0,31},{1,0},{2,1},{3,2},{4,3},{5,4},{6,5},{7,6},{8,7},{9,8},{10,9... | collective-permute-start | bytes 264200 | tf_op jit(solution)/shard_map/ppermute | solution.py:225
  36.7 0.0 collective-permute-start.3
  36.7 2.0 %pad_maximum_fusion = f32[256,640]{1,0:T(8,128)} fusion(f32[256,256]{1,0:T(8,128)} %get-tuple-element.17, f32[256,128]{1,0:T(8,128)} %get-tuple-element.16, f32[256,256]{1,0:T(8,128)} %get-tuple-element.15), kind=kLoop, calls=%fused_computation.3 | loop fusion | flops 327680 | bytes 1310720 | tf_op jit(solution)/shard_map/concatenate | solution.py:231
  38.7 0.0 all-reduce.2.cloned.1.call-update
  38.8 0.8 copy-done.1
  39.6 0.0 copy-done.4
  39.6 0.2 fusion.3
  39.8 0.0 collective-permute-done.2
  39.8 0.7 copy-done
  40.5 0.1 copy-done.2
  40.6 0.9 fusion.1
  41.4 144.8 %all-reduce.2.cloned.1.call-done = f32[256,640]{1,0:T(8,128)} async-done(((f32[256,640]{1,0:T(8,128)}), f32[256,640]{1,0:T(8,128)}) %all-reduce.2.cloned.1.call-update) | async-done | bytes 655376 | tf_op jit(solution)/shard_map/psum | solution.py:232
  186.2 1.1 broadcast_multiply_fusion
  187.3 0.7 slice.13
  188.0 0.8 fusion.2
  (7 shorter events, 0.0 us)
Async XLA Ops:
  7.2 4.2 %copy-start.3 = (bf16[1,256,172]{1,2,0:T(8,128)(2,1)S(1)}, bf16[1,256,172]{1,2,0:T(8,128)(2,1)}, u32[]{:S(2)}) copy-start(bf16[1,256,172]{1,2,0:T(8,128)(2,1)} %param.10) | copy-start | bytes 264196
  7.2 179.0 %all-reduce.2.cloned.1.call-start = ((), (), s32[]{:S(2)}) async-start(), calls=%async_computation | async-start | bytes 1310720 | tf_op jit(solution)/shard_map/psum | solution.py:232
  8.2 5.7 %collective-permute-start.1 = (bf16[256,172]{1,0:T(8,128)(2,1)S(1)}, bf16[256,172]{1,0:T(8,128)(2,1)S(1)}, u32[]{:S(2)}, u32[]{:S(2)}) collective-permute-start(bf16[256,172]{1,0:T(8,128)(2,1)S(1)} %bitcast.13), channel_id=1, source_target_pairs={{0,31},{1,0},{2,1},{3,2},{4,3},{5,4},{6,5},{7,6},{8,7},{9,8},{10,9... | collective-permute-start | bytes 264200 | tf_op jit(solution)/shard_map/ppermute | solution.py:220
  9.7 6.6 %collective-permute-start = (bf16[256,172]{1,0:T(8,128)(2,1)S(1)}, bf16[256,172]{1,0:T(8,128)(2,1)S(1)}, u32[]{:S(2)}, u32[]{:S(2)}) collective-permute-start(bf16[256,172]{1,0:T(8,128)(2,1)S(1)} %bitcast.14), channel_id=1, source_target_pairs={{0,1},{1,2},{2,3},{3,4},{4,5},{5,6},{6,7},{7,8},{8,9},{9,10},{10,1... | collective-permute-start | bytes 264200 | tf_op jit(solution)/shard_map/ppermute | solution.py:219
  29.9 9.9 %collective-permute-start.2 = (bf16[256,172]{1,0:T(8,128)(2,1)}, bf16[256,172]{1,0:T(8,128)(2,1)S(1)}, u32[]{:S(2)}, u32[]{:S(2)}) collective-permute-start(bf16[256,172]{1,0:T(8,128)(2,1)} %get-tuple-element.12), channel_id=1, source_target_pairs={{0,31},{1,0},{2,1},{3,2},{4,3},{5,4},{6,5},{7,6},{8,7},{9,8},{10,9... | collective-permute-start | bytes 264200 | tf_op jit(solution)/shard_map/ppermute | solution.py:225
  36.7 3.1 %collective-permute-start.3 = (bf16[256,172]{1,0:T(8,128)(2,1)}, bf16[256,172]{1,0:T(8,128)(2,1)S(1)}, u32[]{:S(2)}, u32[]{:S(2)}) collective-permute-start(bf16[256,172]{1,0:T(8,128)(2,1)} %get-tuple-element.13), channel_id=1, source_target_pairs={{0,1},{1,2},{2,3},{3,4},{4,5},{5,6},{6,7},{7,8},{8,9},{9,10},{10,1... | collective-permute-start | bytes 264200 | tf_op jit(solution)/shard_map/ppermute | solution.py:226
  38.7 0.8 copy-start.1
  38.7 0.9 copy-start.4
  39.6 0.9 copy-start
  39.6 1.0 copy-start.2
Sparse Core Ops, SparseCore 0:
  38.9 147.2 all-reduce.1

commit v2 on v1

--- a/solution.py
+++ b/solution.py
@@ -1,5 +1,3 @@
-import functools
-
 import jax
 import jax.numpy as jnp
 from jax import lax
@@ -16,6 +14,7 @@
 TAIL = CELLS - 128
 GAP = 128 - 2 * TAIL
 LANES = 384
+COLS = 640
 HEAD = D // HEADS
 PTS = LEVELS * POINTS
 BF = jnp.bfloat16
@@ -26,38 +25,115 @@
     return lax.dot_general(a, b, (((ca,), (cb,)), ((), ())), preferred_element_type=F32)
 
 
-def local_kernel(
+def whole_kernel(
     x_ref,
-    rows_ref,
-    cw_ref,
+    rows_hbm,
+    cw_hbm,
     og_ref,
     vw_ref,
     lw_ref,
     ow_ref,
-    low_ref,
-    own_ref,
-    high_ref,
-    lg_ref,
+    ig_ref,
     gv_ref,
     gl_ref,
     go_ref,
+    rows_ref,
+    cw_ref,
+    halo_s,
     v_s,
     att_s,
     g_s,
     samp_s,
     rep_s,
+    own_s,
     vg_s,
     wide_s,
     m_s,
+    lg_s,
+    back_s,
+    w_s,
+    cs_s,
+    cr_s,
+    ps_s,
+    pr_s,
+    yr_s,
+    ag_s,
+    in_sem,
+    halo_sem,
+    back_sem,
+    core_sem,
+    ps_sem,
+    pr_sem,
+    ys_sem,
+    yr_sem,
+    as_sem,
+    ar_sem,
+    rs_sem,
+    rr_sem,
 ):
     band = lax.axis_index("band")
-    x = x_ref[1]
+    image = lax.axis_index("dp")
+    bands = lax.axis_size("band")
+    images = lax.axis_size("dp")
+    chips = bands // 2
+    core = lax.rem(band, 2)
+    chip = lax.div(band, 2)
+    up = {"band": lax.rem(band + 1, bands)}
+    down = {"band": lax.rem(band + bands - 1, bands)}
+    partner = {"band": band + 1 - 2 * core}
+
+    def peer(t):
+        return lax.rem(chip + t, chips)
+
+    def remote(src, dst, send, recv, where):
+        return pltpu.make_async_remote_copy(
+            src_ref=src,
+            dst_ref=dst,
+            send_sem=send,
+            recv_sem=recv,
+            device_id=where,
+            device_id_type=pl.DeviceIdType.MESH,
+        )
+
+    def each(low, high, step):
+        def run(t, carry):
+            step(t)
+            return carry
+
+        lax.fori_loop(low, high, run, 0)
+
+    barrier = pltpu.get_barrier_semaphore()
+
+    def greet(where):
+        pl.semaphore_signal(barrier, inc=1, device_id=where, device_id_type=pl.DeviceIdType.MESH)
+
+    greet(up)
+    greet(down)
+    each(1, chips, lambda t: greet({"band": 2 * peer(t) + core}))
+    each(1, images, lambda t: greet({"dp": lax.rem(image + t, images)}))
+    rows_in = pltpu.make_async_copy(rows_hbm, rows_ref, in_sem.at[0])
+    cw_in = pltpu.make_async_copy(cw_hbm, cw_ref, in_sem.at[1])
+    rows_in.start()
+    cw_in.start()
+
+    x = x_ref[...]
     og = og_ref[...]
-    for j in range(3):
-        v_s[j] = dot(vw_ref[...], x_ref[j], 0, 0).astype(BF)
+    v_s[1] = dot(vw_ref[...], x, 0, 0).astype(BF)
     logits = dot(lw_ref[...], x, 0, 0)
     att_s[...] = logits.reshape(HEADS, PTS, CELLS)
     g_s[...] = dot(ow_ref[...], og).astype(BF).astype(F32)
+
+    pl.semaphore_wait(barrier, 2 + chips - 1 + images - 1)
+    halo_up = remote(x_ref, halo_s.at[0], halo_sem.at[0], halo_sem.at[2], up)
+    halo_down = remote(x_ref, halo_s.at[1], halo_sem.at[1], halo_sem.at[3], down)
+    halo_up.start()
+    halo_down.start()
+    rows_in.wait()
+    cw_in.wait()
+    halo_up.wait()
+    halo_down.wait()
+    v_s[0] = dot(vw_ref[...], halo_s[0], 0, 0).astype(BF)
+    v_s[2] = dot(vw_ref[...], halo_s[1], 0, 0).astype(BF)
 
     def packed(first, second, rows):
         tail = jnp.concatenate(
@@ -129,7 +205,10 @@
         for j in range(3):
             m_j = m_s[j, :CELLS, :]
             samp = samp + dot(v_s[j, hs, :], m_j)
-            vg_s[j, hs, :] = dot(gp, m_j, 1, 1).astype(BF)
+            part = dot(gp, m_j, 1, 1)
+            if j == 1:
+                own_s[hs, :] = part
+            vg_s[j, hs, :] = part.astype(BF)
         s0 = jnp.concatenate([samp[:HEAD, :128], samp[:HEAD, 256 : 256 + TAIL]], axis=1)
         s1 = jnp.concatenate(
             [samp[HEAD:, 128:256], samp[HEAD:, 256 + TAIL : 256 + 2 * TAIL]], axis=1
@@ -166,78 +245,168 @@
         l0 = jnp.concatenate([lgs[0], lgs[2][:, :TAIL]], axis=1)
         l1 = jnp.concatenate([lgs[1], lgs[2][:, TAIL : 2 * TAIL]], axis=1)
         ks = pl.ds(pl.multiple_of(i * 2 * PTS, 2 * PTS), 2 * PTS)
-        lg_ref[ks, :] = jnp.concatenate([l0, l1], axis=0).astype(BF)
+        lg_s[ks, :] = jnp.concatenate([l0, l1], axis=0).astype(BF)
         return carry
 
     lax.fori_loop(0, HEADS // 2, pair, 0)
-    low_ref[...] = vg_s[0]
-    own_ref[...] = vg_s[1]
-    high_ref[...] = vg_s[2]
-    gv = dot(x_ref[0], vg_s[0], 1, 1)
+    back_down = remote(vg_s.at[0], back_s.at[1], back_sem.at[0], back_sem.at[2], down)
+    back_up = remote(vg_s.at[2], back_s.at[0], back_sem.at[1], back_sem.at[3], up)
+    back_down.start()
+    back_up.start()
+
+    gv = dot(halo_s[0], vg_s[0], 1, 1)
     gv = gv + dot(x, vg_s[1], 1, 1)
-    gv = gv + dot(x_ref[2], vg_s[2], 1, 1)
-    gv_ref[...] = gv
-    gl_ref[...] = dot(x, lg_ref[...], 1, 1)
-    go_ref[...] = dot(samp_s[...], og, 1, 1)
-
-
-def local_pass(x3, rows, cw, og, vw, lw, ow):
+    gv = gv + dot(halo_s[1], vg_s[2], 1, 1)
+    w_s[:, :D] = gv
+    w_s[:, D : D + 128] = dot(x, lg_s[...], 1, 1)
+    w_s[:, D + 128 :] = dot(samp_s[...], og, 1, 1)
+
+    mine = pl.ds(pl.multiple_of(core * 128, 128), 128)
+    other = pl.ds(pl.multiple_of(128 - core * 128, 128), 128)
+    cs_s[...] = w_s[other, :].astype(BF)
+    swap = remote(cs_s, cr_s, core_sem.at[0], core_sem.at[1], partner)
+    swap.start()
+    swap.wait()
+    half = w_s[mine, :] + cr_s[...].astype(F32)
+    w_s[mine, :] = half
+    ps_s[...] = half.astype(BF).reshape(16, 8, COLS)
+
+    def spread(t):
+        q = peer(t)
+        return remote(
+            ps_s.at[q], pr_s.at[chip], ps_sem.at[t], pr_sem.at[chip], {"band": 2 * q + core}
+        )
+
+    def gathered(t):
+        q = peer(t)
+        return remote(
+            ps_s.at[q], pr_s.at[q], ps_sem.at[t], pr_sem.at[q], {"band": 2 * q + core}
+        )
+
+    each(1, chips, lambda t: spread(t).start())
+
+    back_down.wait()
+    back_up.wait()
+    value_grad = own_s[...] + back_s[0].astype(F32) + back_s[1].astype(F32)
+    input_grad = dot(vw_ref[...], value_grad.astype(BF)) + dot(lw_ref[...], lg_s[...])
+    ig_ref[...] = input_grad.astype(BF)
+
+    def add(t, total):
+        gathered(t).wait_recv()
+        return total + pr_s[peer(t)].astype(F32)
+
+    at = pl.multiple_of(core * 128 + chip * 8, 8)
+    total = lax.fori_loop(1, chips, add, w_s[pl.ds(at, 8), :])
+    yr_s[image] = total
+
+    def across(t, slot):
+        q = lax.rem(image + t, images)
+        return remote(
+            yr_s.at[image], yr_s.at[q if slot else image], ys_sem.at[t],
+            yr_sem.at[q if slot else image], {"dp": q},
+        )
+
+    each(1, images, lambda t: across(t, False).start())
+    each(1, images, lambda t: across(t, True).wait_recv())
+    total = yr_s[0]
+    for n in range(1, images):
+        total = total + yr_s[n]
+    scale = 1.0 / float(images * bands * CELLS) ** 0.5
+    ag_s[core, chip] = (total * scale).astype(BF)
+
+    def share(t):
+        q = peer(t)
+        spot = ag_s.at[core, chip]
+        return remote(spot, spot, as_sem.at[t], ar_sem.at[chip], {"band": 2 * q + core})
+
+    def shared(t):
+        q = peer(t)
+        spot = ag_s.at[core, q]
+        return remote(spot, spot, as_sem.at[t], ar_sem.at[q], {"band": 2 * q + core})
+
+    def relay(t):
+        q = peer(t)
+        spot = ag_s.at[core, q]
+        return remote(spot, spot, rs_sem.at[q], rr_sem.at[q], partner)
+
+    def relayed(t):
+        q = peer(t)
+        spot = ag_s.at[1 - core, q]
+        return remote(spot, spot, rs_sem.at[q], rr_sem.at[q], partner)
+
+    each(1, chips, lambda t: share(t).start())
+    relay(0).start()
+
+    def forward(t):
+        shared(t).wait_recv()
+        relay(t).start()
+
+    each(1, chips, forward)
+    each(0, chips, lambda t: relayed(t).wait_recv())
+    whole = ag_s[...].reshape(D, COLS).astype(F32)
+    gv_ref[...] = whole[:, :D]
+    gl_ref[...] = whole[:, D : D + 128]
+    go_ref[...] = whole[:, D + 128 :]
+
+    each(1, chips, lambda t: spread(t).wait_send())
+    each(1, images, lambda t: across(t, False).wait_send())
+    each(1, chips, lambda t: share(t).wait_send())
+    each(0, chips, lambda t: relay(t).wait_send())
+
+
+def body(features, corner_rows, corner_weights, out_grad, vw, lw, ow):
     vm = pl.BlockSpec(memory_space=pltpu.VMEM)
-    return pl.pallas_call(
-        local_kernel,
+    hbm = pl.BlockSpec(memory_space=pl.ANY)
+    dma = pltpu.SemaphoreType.DMA
+    ig, gv, gl, go = pl.pallas_call(
+        whole_kernel,
         out_shape=(
             jax.ShapeDtypeStruct((D, CELLS), BF),
-            jax.ShapeDtypeStruct((D, CELLS), BF),
-            jax.ShapeDtypeStruct((D, CELLS), BF),
-            jax.ShapeDtypeStruct((HEADS * PTS, CELLS), BF),
             jax.ShapeDtypeStruct((D, D), F32),
             jax.ShapeDtypeStruct((D, HEADS * PTS), F32),
             jax.ShapeDtypeStruct((D, D), F32),
         ),
-        in_specs=[vm] * 7,
-        out_specs=[vm] * 7,
+        in_specs=[vm, hbm, hbm, vm, vm, vm, vm],
+        out_specs=[vm] * 4,
         scratch_shapes=[
+            pltpu.VMEM((HEADS, 64, CELLS), jnp.int32),
+            pltpu.VMEM((HEADS, 64, CELLS), F32),
+            pltpu.VMEM((2, D, CELLS), BF),
             pltpu.VMEM((3, D, CELLS), BF),
             pltpu.VMEM((HEADS, PTS, CELLS), F32),
             pltpu.VMEM((D, CELLS), F32),
             pltpu.VMEM((D, CELLS), BF),
             pltpu.VMEM((64, 128), F32),
+            pltpu.VMEM((D, CELLS), F32),
             pltpu.VMEM((3, D, CELLS), BF),
             pltpu.VMEM((4, 64, LANES), F32),
             pltpu.VMEM((3, PAD, LANES), BF),
+            pltpu.VMEM((HEADS * PTS, CELLS), BF),
+            pltpu.VMEM((2, D, CELLS), BF),
+            pltpu.VMEM((D, COLS), F32),
+            pltpu.VMEM((128, COLS), BF),
+            pltpu.VMEM((128, COLS), BF),
+            pltpu.VMEM((16, 8, COLS), BF),
+            pltpu.VMEM((16, 8, COLS), BF),
+            pltpu.VMEM((4, 8, COLS), F32),
+            pltpu.VMEM((2, 16, 8, COLS), BF),
+            dma((2,)),
+            dma((4,)),
+            dma((4,)),
+            dma((2,)),
+            dma((16,)),
+            dma((16,)),
+            dma((4,)),
+            dma((4,)),
+            dma((16,)),
+            dma((16,)),
+            dma((16,)),
+            dma((16,)),
         ],
-        name="local_pass",
-    )(x3, rows, cw, og, vw, lw, ow)
-
-
-def body(features, corner_rows, corner_weights, out_grad, vw, lw, ow):
-    x = features[0]
-    og = out_grad[0]
-    count = lax.axis_size("band")
-    up = [(i, (i + 1) % count) for i in range(count)]
-    down = [(i, (i - 1) % count) for i in range(count)]
-    below = lax.ppermute(x, "band", up)
-    above = lax.ppermute(x, "band", down)
-    x3 = jnp.stack([below, x, above])
-    low, own, high, lg, gv, gl, go = local_pass(
-        x3, corner_rows[0], corner_weights[0], og, vw, lw, ow
-    )
-    from_above = lax.ppermute(low, "band", down)
-    from_below = lax.ppermute(high, "band", up)
-    value_grad = (
-        own.astype(F32) + from_above.astype(F32) + from_below.astype(F32)
-    ).astype(BF)
-    input_grad = dot(vw, value_grad) + dot(lw, lg)
-    flat = jnp.concatenate([gv, gl, go], axis=1)
-    total = lax.psum(flat, ("dp", "band"))
-    scale = 1.0 / float(lax.axis_size("dp") * count * CELLS) ** 0.5
-    total = total * scale
-    return (
-        input_grad.astype(BF)[None],
-        total[:, :D],
-        total[:, D : D + HEADS * PTS],
-        total[:, D + HEADS * PTS :],
-    )
+        compiler_params=pltpu.CompilerParams(collective_id=0, has_side_effects=True),
+        name="whole",
+    )(features[0], corner_rows[0], corner_weights[0], out_grad[0], vw, lw, ow)
+    return (ig[None], gv, gl, go)
 
 
 def solution(mesh):

time: 196 us -> 52.5 us (0.27)
  waiting for transfers between devices: 149 us -> 0 us
  Pallas kernels: 12.7 us -> 44.1 us
  between operations: 14.1 us -> 0.65 us
  starting transfers between devices: 10.1 us -> 0 us
  other arithmetic: 3.96 us -> 0 us
  local copies, waits for them, and re-layouts: 4.84 us -> 7.5 us
    psum x1 -> x0, waiting for transfers between devices: 145 us -> none  [body(): total = lax.psum(flat, ('dp', 'band'))]
    pallas_call x1, Pallas kernels: 12.7 us -> 44.1 us  [body(): pl.pallas_call(whole_kernel, out_shape=(jax.ShapeDtypeStruct((D, CELLS),...]
    ppermute x4 -> x0, starting transfers between devices: 10 us -> none  [the longest x1 6.87 us: body(): from_above = lax.ppermute(low, 'band', down)]
    unnamed x12, local copies, waits for them, and re-layouts: 3.34 us -> 7.5 us
    ppermute x4 -> x0, waiting for transfers between devices: 4.15 us -> none  [the longest x1 2.34 us: body(): below = lax.ppermute(x, 'band', up)]
    concatenate x1 -> x0, other arithmetic: 1.99 us -> none  [body(): flat = jnp.concatenate([gv, gl, go], axis=1)]
  transfers between devices with their start and end apart: 5 -> 0, of which waited for: 3 -> 0; matrix products, arithmetic and copies ran while one was open for 2% -> 0% of each run, Pallas kernels for 0% -> 0%
where the time goes in v2:
time: 52.5 us; the launch traced here: 52.2 us
  Pallas kernels  44.1 us (84%)
  local copies, waits for them, and re-layouts  7.5 us (14%)
  between operations  0.65 us (1%)
    pallas_call x1, Pallas kernels, body(): pl.pallas_call(whole_kernel, out_shape=(jax.ShapeDtypeStruct((D, CELLS),...  44.1 us
    unnamed x12, local copies, waits for them, and re-layouts  7.5 us

profile of v2, /device:TPU:1, one launch (start us, length us, event | category | flops | bytes accessed | tf_op | source)
XLA Modules:
  0.0 52.2 jit_solution(16121858846728215723)
XLA Ops:
  0.6 0.0 copy-start.2
  0.6 1.7 %copy.11 = bf16[1,256,172]{2,1,0:T(8,128)(2,1)} copy(bf16[1,256,172]{1,2,0:T(8,128)(2,1)} %param.7) | data formatting | bytes 176128 | tf_op args[0]
  2.3 0.0 copy-done.2
  2.3 0.8 %copy.12 = bf16[1,256,172]{2,1,0:T(8,128)(2,1)} copy(bf16[1,256,172]{1,2,0:T(8,128)(2,1)S(1)} %copy-done.2) | data formatting | bytes 176128 | tf_op args[3]
  3.1 44.1 %whole.1 = (bf16[256,172]{1,0:T(8,128)(2,1)}, f32[256,256]{1,0:T(8,128)}, f32[256,128]{1,0:T(8,128)}, f32[256,256]{1,0:T(8,128)}) custom-call(bf16[256,172]{1,0:T(8,128)(2,1)} %bitcast.7, s32[8,64,172]{2,1,0:T(8,128)} %bitcast.5, f32[8,64,172]{2,1,0:T(8,128)} %bitcast.6, bf16[256,172]{1,0:T(8,128)(2,1)} %bitcast.8, bf16[256,256]{1,0:T(8,128)(2,1)} %vw_ref.1, ...), custom_call_target="tpu_custom_call" | custom-call | tf_op jit(solution)/shard_map/whole/pallas_call | solution.py:361
  47.2 1.6 %copy.13 = bf16[1,256,172]{1,2,0:T(8,128)(2,1)} copy(bf16[1,256,172]{2,1,0:T(8,128)(2,1)} %bitcast.9) | data formatting | bytes 176128
  48.8 0.0 copy-start.1
  48.8 1.7 %copy.17 = f32[256,256]{1,0:T(8,128)} copy(f32[256,256]{1,0:T(8,128)} %get-tuple-element.21) | data formatting | bytes 524288
  50.5 0.0 copy-done.1
  50.5 0.0 copy-start
  50.5 0.7 %copy.18 = f32[256,128]{1,0:T(8,128)} copy(f32[256,128]{1,0:T(8,128)S(1)} %copy-done.1) | data formatting | bytes 262144
  51.2 0.3 copy-done
  51.5 0.7 %copy.19 = f32[256,256]{1,0:T(8,128)} copy(f32[256,256]{1,0:T(8,128)S(1)} %copy-done) | data formatting | bytes 524288
Async XLA Ops:
  0.6 1.7 %copy-start.2 = (bf16[1,256,172]{1,2,0:T(8,128)(2,1)S(1)}, bf16[1,256,172]{1,2,0:T(8,128)(2,1)}, u32[]{:S(2)}) copy-start(bf16[1,256,172]{1,2,0:T(8,128)(2,1)} %param.10) | copy-start | bytes 264196
  48.8 1.7 %copy-start.1 = (f32[256,128]{1,0:T(8,128)S(1)}, f32[256,128]{1,0:T(8,128)}, u32[]{:S(2)}) copy-start(f32[256,128]{1,0:T(8,128)} %get-tuple-element.22) | copy-start | bytes 393220
  50.5 1.0 %copy-start = (f32[256,256]{1,0:T(8,128)S(1)}, f32[256,256]{1,0:T(8,128)}, u32[]{:S(2)}) copy-start(f32[256,256]{1,0:T(8,128)} %get-tuple-element.23) | copy-start | bytes 786436

commit v3 on v2

v3 whole, which is shorter than its diff:
```python
import jax
import jax.numpy as jnp
from jax import lax
from jax.experimental import pallas as pl
from jax.experimental.pallas import tpu as pltpu
from jax.sharding import PartitionSpec as P

HEADS = 8
LEVELS = 4
POINTS = 4
D = 256
CELLS = 172
PAD = 176
TAIL = CELLS - 128
GAP = 128 - 2 * TAIL
LANES = 384
PAIRS = HEADS // 2
HEAD = D // HEADS
PTS = LEVELS * POINTS
ROWS = 2 * D + HEADS * PTS
PIECE = 40
BF = jnp.bfloat16
F32 = jnp.float32
I32 = jnp.int32


def dot(a, b, ca=1, cb=0):
    return lax.dot_general(a, b, (((ca,), (cb,)), ((), ())), preferred_element_type=F32)


def lane_pick(table, index):
    numbers = lax.GatherDimensionNumbers(
        offset_dims=(),
        collapsed_slice_dims=(1,),
        start_index_map=(1,),
        operand_batching_dims=(0,),
        start_indices_batching_dims=(0,),
    )
    return lax.gather(
        table,
        index[..., None],
        numbers,
        slice_sizes=(1, 1),
        mode=lax.GatherScatterMode.PROMISE_IN_BOUNDS,
    )


def whole_kernel(
    x_hbm,
    rows_hbm,
    cw_hbm,
    og_hbm,
    vw_hbm,
    lw_hbm,
    ow_hbm,
    ig_ref,
    ag_ref,
    x_s,
    og_s,
    vw_s,
    lw_s,
    ow_s,
    rows_s,
    cw_s,
    vwt_s,
    halo_s,
    v_s,
    att_s,
    g_s,
    samp_s,
    rep_s,
    own_s,
    vg_s,
    wide_s,
    m_s,
    lg_s,
    send_s,
    back_s,
    w_s,
    cs_s,
    cr_s,
    ps_s,
    pr_s,
    yr_s,
    in_sem,
    halo_sem,
    back_sem,
    core_sem,
    ps_sem,
    pr_sem,
    ys_sem,
    yr_sem,
    as_sem,
    ar_sem,
    rs_sem,
    rr_sem,
):
    band = lax.axis_index("band")
    image = lax.axis_index("dp")
    bands = lax.axis_size("band")
    images = lax.axis_size("dp")
    chips = bands // 2
    core = lax.rem(band, 2)
    chip = lax.div(band, 2)
    up = {"band": lax.rem(band + 1, bands)}
    down = {"band": lax.rem(band + bands - 1, bands)}
    partner = {"band": band + 1 - 2 * core}

    def peer(t):
        return lax.rem(chip + t, chips)

    def remote(src, dst, send, recv, where):
        return pltpu.make_async_remote_copy(
            src_ref=src,
            dst_ref=dst,
            send_sem=send,
            recv_sem=recv,
            device_id=where,
            device_id_type=pl.DeviceIdType.MESH,
        )

    def each(low, high, step):
        def run(t, carry):
            step(t)
            return carry

        lax.fori_loop(low, high, run, 0)

    barrier = pltpu.get_barrier_semaphore()

    def greet(where):
        pl.semaphore_signal(barrier, inc=1, device_id=where, device_id_type=pl.DeviceIdType.MESH)

    loads = [
        pltpu.make_async_copy(src, dst, in_sem.at[n])
        for n, (src, dst) in enumerate(
            [
                (x_hbm, x_s),
                (lw_hbm, lw_s),
                (rows_hbm, rows_s),
                (cw_hbm, cw_s),
                (vw_hbm, vw_s),
                (og_hbm, og_s),
                (ow_hbm, ow_s),
            ]
        )
    ]
    for load in loads:
        load.start()
    greet(up)
    greet(down)
    each(1, chips, lambda t: greet({"band": 2 * peer(t) + core}))
    each(1, images, lambda t: greet({"dp": lax.rem(image + t, images)}))

    loads[0].wait()
    loads[1].wait()
    x = x_s[...]
    att_s[...] = dot(lw_s[...].T, x, 1, 1).reshape(HEADS, PTS, CELLS)
    loads[2].wait()
    loads[3].wait()

    def packed(first, second):
        tail = jnp.concatenate(
            [first[:, 128:], second[:, 128:], jnp.zeros((first.shape[0], GAP), first.dtype)],
            axis=1,
        )
        return [first[:, :128], second[:, :128], tail]

    sub = lax.broadcasted_iota(I32, (16, 128), 0)
    ids = [(sub + cb * 16).astype(F32).astype(BF) for cb in range(11)]
    base = (band - 1) * CELLS
    nil = jnp.zeros((), BF)

    def build(i):
        cells = packed(rows_s[2 * i] - base, rows_s[2 * i + 1] - base)
        cw = packed(cw_s[2 * i], cw_s[2 * i + 1])
        logit = packed(att_s[2 * i], att_s[2 * i + 1])
        att = []
        for g in range(3):
            e = jnp.exp(logit[g])
            att.append(e / jnp.sum(e, axis=0, keepdims=True))
            rep = rep_s.at[(i % 2) * 6 + g]
            for c in range(4):
                rep[pl.ds(c, PTS, stride=4), :] = att[g]
            over1 = cells[g] >= CELLS
            over2 = cells[g] >= 2 * CELLS
            r = cells[g] - jnp.where(over2, 2 * CELLS, jnp.where(over1, CELLS, 0))
            w = (rep[...] * cw[g]).astype(BF).astype(F32)
            zero = jnp.zeros_like(w)
            wide = wide_s.at[i % 2, g]
            wide[0] = r.astype(F32)
            wide[1] = jnp.where(over1, zero, w)
            wide[2] = jnp.where(over1, jnp.where(over2, zero, w), zero)
            wide[3] = jnp.where(over2, w, zero)
            for cbs, levels in ((range(8), (0,)), (range(8, 10), (1,)), (range(10, 11), (2, 3))):
                acc = [[None] * 3 for _ in cbs]
                for lev in levels:
                    for k in range(lev * 16, lev * 16 + 16):
                        row = [
                            jnp.broadcast_to(wide[n, pl.ds(k, 1), :], (16, 128)).astype(BF)
                            for n in range(4)
                        ]
                        for at, cb in enumerate(cbs):
                            hit = row[0] == ids[cb]
                            for j in range(3):
                                term = jnp.where(hit, row[1 + j], nil)
                                old = acc[at][j]
                                acc[at][j] = term if old is None else old + term
                for at, cb in enumerate(cbs):
                    for j in range(3):
                        m_s[i, j, cb * 16 : cb * 16 + 16, g * 128 : (g + 1) * 128] = acc[at][j]
        return cells, cw, att

    def project(i, built):
        cells, cw, att = built
        hs = slice(i * 2 * HEAD, (i + 1) * 2 * HEAD)
        g0 = g_s[i * 2 * HEAD : i * 2 * HEAD + HEAD, :]
        g1 = g_s[i * 2 * HEAD + HEAD : (i + 1) * 2 * HEAD, :]
        none = jnp.zeros((HEAD, 128), F32)
        top = [
            g0[:, :128],
            none,
            jnp.concatenate([g0[:, 128:], none[:, : 128 - TAIL]], axis=1),
        ]
        bottom = [
            none,
            g1[:, :128],
            jnp.concatenate([none[:, :TAIL], g1[:, 128:], none[:, : 128 - 2 * TAIL]], axis=1),
        ]
        gp = jnp.concatenate(
            [jnp.concatenate(top, axis=1), jnp.concatenate(bottom, axis=1)], axis=0
        ).astype(BF)
        samp = jnp.zeros((2 * HEAD, LANES), F32)
        for j in range(3):
            m_j = m_s[i, j, :CELLS, :]
            samp = samp + dot(v_s[j, hs, :], m_j)
            part = dot(gp, m_j, 1, 1)
            if j == 1:
                own_s[hs, :] = part
            vg_s[j, hs, :] = part.astype(BF)
        s0 = jnp.concatenate([samp[:HEAD, :128], samp[:HEAD, 256 : 256 + TAIL]], axis=1)
        s1 = jnp.concatenate(
            [samp[HEAD:, 128:256], samp[HEAD:, 256 + TAIL : 256 + 2 * TAIL]], axis=1
        )
        samp_s[hs, :] = jnp.concatenate([s0, s1], axis=0).astype(BF)

        lgs = []
        for g in range(3):
            at = jnp.concatenate([cells[g], jnp.zeros((64, 128), I32)], axis=0).T
            over1 = at >= CELLS
            over2 = at >= 2 * CELLS
            r = at - jnp.where(over2, 2 * CELLS, jnp.where(over1, CELLS, 0))
            index = jnp.bitwise_and(r, 127)
            near = r < 128
            g_t = jnp.concatenate([top[g], bottom[g]], axis=0).T.astype(BF)
            pick = None
            for j in range(3):
                score = dot(g_t, v_s[j, hs, :])
                tail = jnp.concatenate([score[:, 128:], jnp.zeros((128, 256 - CELLS), F32)], axis=1)
                val = jnp.where(near, lane_pick(score[:, :128], index), lane_pick(tail, index))
                if j == 0:
                    pick = val
                elif j == 1:
                    pick = jnp.where(over1, val, pick)
                else:
                    pick = jnp.where(over2, val, pick)
            rep = rep_s.at[(i % 2) * 6 + 3 + g]
            rep[...] = pick.T[:64] * cw[g]
            ag = jnp.zeros((PTS, 128), F32)
            for c in range(4):
                ag = ag + rep[pl.ds(c, PTS, stride=4), :]
            lgs.append(att[g] * (ag - jnp.sum(att[g] * ag, axis=0, keepdims=True)))
        l0 = jnp.concatenate([lgs[0], lgs[2][:, :TAIL]], axis=1)
        l1 = jnp.concatenate([lgs[1], lgs[2][:, TAIL : 2 * TAIL]], axis=1)
        lg_s[i * 2 * PTS : (i + 1) * 2 * PTS, :] = jnp.concatenate([l0, l1], axis=0).astype(BF)

    built = [build(0)]

    pl.semaphore_wait(barrier, 2 + chips - 1 + images - 1)
    halo_up = remote(x_s, halo_s.at[0], halo_sem.at[0], halo_sem.at[2], up)
    halo_down = remote(x_s, halo_s.at[1], halo_sem.at[1], halo_sem.at[3], down)
    halo_up.start()
    halo_down.start()

    for load in loads[4:]:
        load.wait()
    built.append(build(1))
    vwt_s[...] = vw_s[...].T
    og = og_s[...]
    g_s[...] = dot(ow_s[...], og, 1, 1).astype(BF).astype(F32)
    v_s[1] = dot(vwt_s[...], x, 1, 1).astype(BF)

    halo_up.wait()
    halo_down.wait()

    v_s[0] = dot(vwt_s[...], halo_s[0], 1, 1).astype(BF)
    v_s[2] = dot(vwt_s[...], halo_s[1], 1, 1).astype(BF)
    for i in range(PAIRS):
        project(i, built[i])
        if i + 2 < PAIRS:
            built.append(build(i + 2))

    send_s[0] = vg_s[0].T
    send_s[1] = vg_s[2].T
    back_down = remote(send_s.at[0], back_s.at[1], back_sem.at[0], back_sem.at[2], down)
    back_up = remote(send_s.at[1], back_s.at[0], back_sem.at[1], back_sem.at[3], up)
    back_down.start()
    back_up.start()

    gv = dot(vg_s[0], halo_s[0])
    gv = gv + dot(vg_s[1], x)
    gv = gv + dot(vg_s[2], halo_s[1])
    gl = dot(lg_s[...], x)
    go = dot(samp_s[...], og)
    for c in range(2):
        cols = slice(c * 128, (c + 1) * 128)
        w_s[c, :D, :] = gv[:, cols]
        w_s[c, D : D + HEADS * PTS, :] = gl[:, cols]
        w_s[c, D + HEADS * PTS :, :] = go[:, cols]

    cs_s[...] = w_s[1 - core].astype(BF)
    swap = remote(cs_s, cr_s, core_sem.at[0], core_sem.at[1], partner)
    swap.start()
    swap.wait()
    half = w_s[core] + cr_s[...].astype(F32)
    w_s[core] = half
    ps_s[...] = half.astype(BF).reshape(16, PIECE, 128)

    def spread(t):
        q = peer(t)
        return remote(
            ps_s.at[q], pr_s.at[chip], ps_sem.at[t], pr_sem.at[chip], {"band": 2 * q + core}
        )

    def gathered(t):
        q = peer(t)
        return remote(ps_s.at[q], pr_s.at[q], ps_sem.at[t], pr_sem.at[q], {"band": 2 * q + core})

    each(1, chips, lambda t: spread(t).start())

    back_down.wait()
    back_up.wait()
    value_grad = own_s[...].T + back_s[0].astype(F32) + back_s[1].astype(F32)
    input_grad = dot(value_grad.astype(BF), vwt_s[...]) + dot(
        lg_s[...].astype(F32).T.astype(BF), lw_s[...], 1, 1
    )
    ig_ref[...] = input_grad.astype(BF)

    def add(t, total):
        gathered(t).wait_recv()
        return total + pr_s[peer(t)].astype(F32)

    at = pl.multiple_of(chip * PIECE, 8)
    total = lax.fori_loop(1, chips, add, w_s[core, pl.ds(at, PIECE), :])

    yr_s[image] = total

    def across(t, slot):
        q = lax.rem(image + t, images)
        n = q if slot else image
        return remote(yr_s.at[image], yr_s.at[n], ys_sem.at[t], yr_sem.at[n], {"dp": q})

    each(1, images, lambda t: across(t, False).start())
    each(1, images, lambda t: across(t, True).wait_recv())
    total = yr_s[0]
    for n in range(1, images):
        total = total + yr_s[n]
    scale = 1.0 / float(images * bands * CELLS) ** 0.5
    ag_ref[core, chip] = (total * scale).astype(BF)

    def share(t, slot):
        q = peer(t)
        spot = ag_ref.at[core, q if slot else chip]
        return remote(
            spot, spot, as_sem.at[t], ar_sem.at[q if slot else chip], {"band": 2 * q + core}
        )

    def relay(t, side):
        q = peer(t)
        spot = ag_ref.at[side, q]
        return remote(spot, spot, rs_sem.at[q], rr_sem.at[q], partner)

    each(1, chips, lambda t: share(t, False).start())
    relay(0, core).start()

    def forward(t):
        share(t, True).wait_recv()
        relay(t, core).start()

    each(1, chips, forward)
    each(0, chips, lambda t: relay(t, 1 - core).wait_recv())

    each(1, chips, lambda t: spread(t).wait_send())
    each(1, images, lambda t: across(t, False).wait_send())
    each(1, chips, lambda t: share(t, False).wait_send())
    each(0, chips, lambda t: relay(t, core).wait_send())


def finish_kernel(ag_ref, ig_in, ig_ref, gv_ref, gl_ref, go_ref):
    ig_ref[...] = ig_in[...]
    for c in range(2):
        cols = slice(c * 128, (c + 1) * 128)
        part = ag_ref[c].reshape(ROWS, 128).astype(F32)
        gv_ref[cols, :] = part[:D].T
        gl_ref[cols, :] = part[D : D + HEADS * PTS].T
        go_ref[:, cols] = part[D + HEADS * PTS :]


def body(features, corner_rows, corner_weights, out_grad, vw, lw, ow):
    vm = pl.BlockSpec(memory_space=pltpu.VMEM)
    hbm = pl.BlockSpec(memory_space=pltpu.HBM)
    dma = pltpu.SemaphoreType.DMA
    ig, ag = pl.pallas_call(
        whole_kernel,
        out_shape=(
            pltpu.VMEM((CELLS, D), BF),
            pltpu.VMEM((2, 16, PIECE, 128), BF),
        ),
        in_specs=[hbm] * 7,
        out_specs=[vm] * 2,
        scratch_shapes=[
            pltpu.VMEM((CELLS, D), BF),
            pltpu.VMEM((CELLS, D), BF),
            pltpu.VMEM((D, D), BF),
            pltpu.VMEM((D, HEADS * PTS), BF),
            pltpu.VMEM((D, D), BF),
            pltpu.VMEM((HEADS, 64, CELLS), I32),
            pltpu.VMEM((HEADS, 64, CELLS), F32),
            pltpu.VMEM((D, D), BF),
            pltpu.VMEM((2, CELLS, D), BF),
            pltpu.VMEM((3, D, CELLS), BF),
            pltpu.VMEM((HEADS, PTS, CELLS), F32),
            pltpu.VMEM((D, CELLS), F32),
            pltpu.VMEM((D, CELLS), BF),
            pltpu.VMEM((12, 64, 128), F32),
            pltpu.VMEM((D, CELLS), F32),
            pltpu.VMEM((3, D, CELLS), BF),
            pltpu.VMEM((2, 3, 4, 64, 128), F32),
            pltpu.VMEM((PAIRS, 3, PAD, LANES), BF),
            pltpu.VMEM((HEADS * PTS, CELLS), BF),
            pltpu.VMEM((2, CELLS, D), BF),
            pltpu.VMEM((2, CELLS, D), BF),
            pltpu.VMEM((2, ROWS, 128), F32),
            pltpu.VMEM((ROWS, 128), BF),
            pltpu.VMEM((ROWS, 128), BF),
            pltpu.VMEM((16, PIECE, 128), BF),
            pltpu.VMEM((16, PIECE, 128), BF),
            pltpu.VMEM((4, PIECE, 128), F32),
            dma((7,)),
            dma((4,)),
            dma((4,)),
            dma((2,)),
            dma((16,)),
            dma((16,)),
            dma((4,)),
            dma((4,)),
            dma((16,)),
            dma((16,)),
            dma((16,)),
            dma((16,)),
        ],
        compiler_params=pltpu.CompilerParams(
            collective_id=0, has_side_effects=True, vmem_limit_bytes=60 * 10**6
        ),
        name="whole",
    )(
        features[0].T,
        corner_rows[0],
        corner_weights[0],
        out_grad[0].T,
        vw,
        lw,
        ow,
    )
    ig, gv, gl, go = pl.pallas_call(
        finish_kernel,
        out_shape=(
            jax.ShapeDtypeStruct((CELLS, D), BF),
            jax.ShapeDtypeStruct((D, D), F32),
            jax.ShapeDtypeStruct((D, HEADS * PTS), F32),
            jax.ShapeDtypeStruct((D, D), F32),
        ),
        in_specs=[vm] * 2,
        out_specs=[vm] * 4,
        compiler_params=pltpu.CompilerParams(vmem_limit_bytes=8 * 2**20),
        name="finish",
    )(ag, ig)
    return (ig.T[None], gv, gl, go)


def solution(mesh):
    placed = (
        P("dp", None, "band"),
        P("dp", None, None, "band"),
        P("dp", None, None, "band"),
        P("dp", None, "band"),
        P(),
        P(),
        P(),
    )
    return jax.shard_map(
        body,
        mesh=mesh,
        in_specs=placed,
        out_specs=(P("dp", None, "band"), P(), P(), P()),
        check_vma=False,
    )
```

time: 52.5 us -> 39.9 us (0.76)
  local copies, waits for them, and re-layouts: 7.5 us -> 0 us
  Pallas kernels: 44.1 us -> 39.1 us
    unnamed x12 -> x0, local copies, waits for them, and re-layouts: 7.5 us -> none
    pallas_call x1 -> x2, Pallas kernels: 44.1 us -> 39.1 us  [the longest x1 38.2 us: body(): pl.pallas_call(whole_kernel, out_shape=(pltpu.VMEM((CELLS, D), BF), pltpu...]
where the time goes in v3:
time: 39.9 us; the launch traced here: 39.7 us
  Pallas kernels  39.1 us (98%)
  between operations  0.64 us (2%)
    pallas_call x1, Pallas kernels, body(): pl.pallas_call(whole_kernel, out_shape=(pltpu.VMEM((CELLS, D), BF), pltpu...  38.2 us
    pallas_call x1, Pallas kernels, body(): pl.pallas_call(finish_kernel, out_shape=(jax.ShapeDtypeStruct((CELLS, D),...  0.92 us

profile of v3, /device:TPU:1, one launch (start us, length us, event | category | flops | bytes accessed | tf_op | source)
XLA Modules:
  0.0 39.7 jit_solution(10204656481448663949)
XLA Ops:
  0.6 38.2 %whole.1 = (bf16[172,256]{1,0:T(8,128)(2,1)S(1)}, bf16[2,16,40,128]{3,2,1,0:T(8,128)(2,1)S(1)}) custom-call(bf16[172,256]{1,0:T(8,128)(2,1)} %bitcast.13, s32[8,64,172]{2,1,0:T(8,128)} %bitcast.11, f32[8,64,172]{2,1,0:T(8,128)} %bitcast.12, bf16[172,256]{1,0:T(8,128)(2,1)} %bitcast.14, bf16[256,256]{1,0:T(8,128)(2,1)} %vw_hbm.1, bf16[256,128]{1,0:T(8,128)(2,1)} %lw_hbm.1, ...), custom_call_target="tpu_custom_call" | custom-call | tf_op jit(solution)/shard_map/whole/pallas_call | solution.py:413
  38.8 0.9 %finish.1 = (bf16[172,256]{1,0:T(8,128)(2,1)}, f32[256,256]{1,0:T(8,128)}, f32[256,128]{1,0:T(8,128)}, f32[256,256]{1,0:T(8,128)}) custom-call(bf16[2,16,40,128]{3,2,1,0:T(8,128)(2,1)S(1)} %get-tuple-element.10.ag_ref, bf16[172,256]{1,0:T(8,128)(2,1)S(1)} %get-tuple-element.11.ig_in), custom_call_target="tpu_custom_call" | custom-call | tf_op jit(solution)/shard_map/finish/pallas_call | solution.py:475

commit v4 on v3

v4 whole, which is shorter than its diff:
```python
import jax
import jax.numpy as jnp
from jax import lax
from jax.experimental import pallas as pl
from jax.experimental.pallas import tpu as pltpu
from jax.sharding import PartitionSpec as P

HEADS = 8
LEVELS = 4
POINTS = 4
D = 256
CELLS = 172
PAD = 176
TAIL = CELLS - 128
GAP = 128 - 2 * TAIL
LANES = 384
PAIRS = HEADS // 2
HEAD = D // HEADS
PTS = LEVELS * POINTS
CHUNKS = (256, 256, 128)
BF = jnp.bfloat16
F32 = jnp.float32
I32 = jnp.int32


def dot(a, b, ca=1, cb=0):
    return lax.dot_general(a, b, (((ca,), (cb,)), ((), ())), preferred_element_type=F32)


def lane_pick(table, index):
    numbers = lax.GatherDimensionNumbers(
        offset_dims=(),
        collapsed_slice_dims=(1,),
        start_index_map=(1,),
        operand_batching_dims=(0,),
        start_indices_batching_dims=(0,),
    )
    return lax.gather(
        table,
        index[..., None],
        numbers,
        slice_sizes=(1, 1),
        mode=lax.GatherScatterMode.PROMISE_IN_BOUNDS,
    )


def whole_kernel(
    x_hbm,
    rows_hbm,
    cw_hbm,
    og_hbm,
    vw_hbm,
    lw_hbm,
    ow_hbm,
    ig_ref,
    aga_ref,
    agb_ref,
    agc_ref,
    x_s,
    og_s,
    vw_s,
    lw_s,
    ow_s,
    rows_s,
    cw_s,
    vwt_s,
    halo_s,
    v_s,
    att_s,
    g_s,
    samp_s,
    rep_s,
    own_s,
    vg_s,
    wide_s,
    m_s,
    lg_s,
    send_s,
    back_s,
    gp_s,
    gt_s,
    half_s,
    at_s,
    pick_s,
    w_s,
    cs_s,
    cr_s,
    ps_s,
    pr_s,
    yr_s,
    in_sem,
    halo_sem,
    back_sem,
    core_sem,
    ps_sem,
    pr_sem,
    ys_sem,
    yr_sem,
    as_sem,
    ar_sem,
    rs_sem,
    rr_sem,
):
    ag_refs = (aga_ref, agb_ref, agc_ref)
    band = lax.axis_index("band")
    image = lax.axis_index("dp")
    bands = lax.axis_size("band")
    images = lax.axis_size("dp")
    chips = bands // 2
    core = lax.rem(band, 2)
    chip = lax.div(band, 2)
    up = {"band": lax.rem(band + 1, bands)}
    down = {"band": lax.rem(band + bands - 1, bands)}
    partner = {"band": band + 1 - 2 * core}

    def peer(t):
        return lax.rem(chip + t, chips)

    def remote(src, dst, send, recv, where):
        return pltpu.make_async_remote_copy(
            src_ref=src,
            dst_ref=dst,
            send_sem=send,
            recv_sem=recv,
            device_id=where,
            device_id_type=pl.DeviceIdType.MESH,
        )

    def each(low, high, step):
        def run(t, carry):
            step(t)
            return carry

        lax.fori_loop(low, high, run, 0)

    barrier = pltpu.get_barrier_semaphore()

    def greet(where):
        pl.semaphore_signal(barrier, inc=1, device_id=where, device_id_type=pl.DeviceIdType.MESH)

    first, rest = pl.ds(0, 2), pl.ds(2, HEADS - 2)
    loads = [
        pltpu.make_async_copy(src, dst, in_sem.at[n])
        for n, (src, dst) in enumerate(
            [
                (x_hbm, x_s),
                (lw_hbm, lw_s),
                (rows_hbm.at[first], rows_s.at[first]),
                (cw_hbm.at[first], cw_s.at[first]),
                (vw_hbm, vw_s),
                (og_hbm, og_s),
                (ow_hbm, ow_s),
                (rows_hbm.at[rest], rows_s.at[rest]),
                (cw_hbm.at[rest], cw_s.at[rest]),
            ]
        )
    ]
    for load in loads:
        load.start()
    each(1, bands, lambda t: greet({"band": lax.rem(band + t, bands)}))
    each(1, images, lambda t: greet({"dp": lax.rem(image + t, images)}))

    loads[0].wait()
    loads[1].wait()
    x = x_s[...]
    att_s[...] = dot(lw_s[...].T, x, 1, 1).reshape(HEADS, PTS, CELLS)
    loads[2].wait()
    loads[3].wait()

    def packed(first, second):
        tail = jnp.concatenate(
            [first[:, 128:], second[:, 128:], jnp.zeros((first.shape[0], GAP), first.dtype)],
            axis=1,
        )
        return [first[:, :128], second[:, :128], tail]

    sub = lax.broadcasted_iota(I32, (16, 128), 0)
    ids = [(sub + cb * 16).astype(F32).astype(BF) for cb in range(11)]
    base = (band - 1) * CELLS
    nil = jnp.zeros((), BF)

    def build(i):
        cells = packed(rows_s[2 * i] - base, rows_s[2 * i + 1] - base)
        cw = packed(cw_s[2 * i], cw_s[2 * i + 1])
        logit = packed(att_s[2 * i], att_s[2 * i + 1])
        att = []
        for g in range(3):
            e = jnp.exp(logit[g])
            att.append(e / jnp.sum(e, axis=0, keepdims=True))
            rep = rep_s.at[(i % 2) * 6 + g]
            for c in range(4):
                rep[pl.ds(c, PTS, stride=4), :] = att[g]
            over1 = cells[g] >= CELLS
            over2 = cells[g] >= 2 * CELLS
            r = cells[g] - jnp.where(over2, 2 * CELLS, jnp.where(over1, CELLS, 0))
            w = (rep[...] * cw[g]).astype(BF).astype(F32)
            zero = jnp.zeros_like(w)
            wide = wide_s.at[i % 2, g]
            wide[0] = r.astype(F32)
            wide[1] = jnp.where(over1, zero, w)
            wide[2] = jnp.where(over1, jnp.where(over2, zero, w), zero)
            wide[3] = jnp.where(over2, w, zero)
            for cbs, levels in ((range(8), (0,)), (range(8, 10), (1,)), (range(10, 11), (2, 3))):
                acc = [[None] * 3 for _ in cbs]
                for lev in levels:
                    for k in range(lev * 16, lev * 16 + 16):
                        row = [
                            jnp.broadcast_to(wide[n, pl.ds(k, 1), :], (16, 128)).astype(BF)
                            for n in range(4)
                        ]
                        for at, cb in enumerate(cbs):
                            hit = row[0] == ids[cb]
                            for j in range(3):
                                term = jnp.where(hit, row[1 + j], nil)
                                old = acc[at][j]
                                acc[at][j] = term if old is None else old + term
                for at, cb in enumerate(cbs):
                    for j in range(3):
                        m_s[i, j, cb * 16 : cb * 16 + 16, g * 128 : (g + 1) * 128] = acc[at][j]
        return cells, cw, att

    def heads_of(i):
        return slice(i * 2 * HEAD, (i + 1) * 2 * HEAD)

    def parts(at):
        over1 = at >= CELLS
        over2 = at >= 2 * CELLS
        r = at - jnp.where(over2, 2 * CELLS, jnp.where(over1, CELLS, 0))
        return over1, over2, r < 128, jnp.bitwise_and(r, 127)

    def spread_grad(i):
        g0 = g_s[i * 2 * HEAD : i * 2 * HEAD + HEAD, :]
        g1 = g_s[i * 2 * HEAD + HEAD : (i + 1) * 2 * HEAD, :]
        none = jnp.zeros((HEAD, 128), F32)
        top = [
            g0[:, :128],
            none,
            jnp.concatenate([g0[:, 128:], none[:, : 128 - TAIL]], axis=1),
        ]
        bottom = [
            none,
            g1[:, :128],
            jnp.concatenate([none[:, :TAIL], g1[:, 128:], none[:, : 128 - 2 * TAIL]], axis=1),
        ]
        for g in range(3):
            both = jnp.concatenate([top[g], bottom[g]], axis=0)
            gp_s[i, :, g * 128 : (g + 1) * 128] = both.astype(BF)
            gt_s[i, g] = both.T.astype(BF)

    def project_own(i):
        hs = heads_of(i)
        m_j = m_s[i, 1, :CELLS, :]
        half_s[i] = dot(v_s[1, hs, :CELLS], m_j)
        part = dot(gp_s[i], m_j, 1, 1)
        own_s[hs, :] = part
        vg_s[1, hs, :] = part.astype(BF)

    def project_beside(i):
        hs = heads_of(i)
        samp = half_s[i]
        for j in (0, 2):
            m_j = m_s[i, j, :CELLS, :]
            samp = samp + dot(v_s[j, hs, :CELLS], m_j)
            vg_s[j, hs, :] = dot(gp_s[i], m_j, 1, 1).astype(BF)
        s0 = jnp.concatenate([samp[:HEAD, :128], samp[:HEAD, 256 : 256 + TAIL]], axis=1)
        s1 = jnp.concatenate(
            [samp[HEAD:, 128:256], samp[HEAD:, 256 + TAIL : 256 + 2 * TAIL]], axis=1
        )
        samp_s[hs, :] = jnp.concatenate([s0, s1], axis=0).astype(BF)

    def lookup(table, near, index):
        near_part = lane_pick(table[:, :128], index)
        return jnp.where(near, near_part, lane_pick(table[:, 128:], index))

    def groups(g):
        return range(0, 128 if g < 2 else 2 * TAIL, 8)

    def attend_own(i, built):
        for g in range(3):
            at = jnp.concatenate([built[0][g], jnp.zeros((64, 128), I32)], axis=0).T
            at_s[i, g] = at
            score = dot(gt_s[i, g], v_s[1, heads_of(i), :])
            for q in groups(g):
                _, _, near, index = parts(at[q : q + 8])
                pick_s[i, g, q : q + 8, :] = lookup(score[q : q + 8], near, index)

    def attend_beside(i, built):
        _, cw, att = built
        lgs = []
        for g in range(3):
            below = dot(gt_s[i, g], v_s[0, heads_of(i), :])
            above = dot(gt_s[i, g], v_s[2, heads_of(i), :])
            for q in groups(g):
                qs = slice(q, q + 8)
                over1, over2, near, index = parts(at_s[i, g, qs, :])
                pick = jnp.where(over1, pick_s[i, g, qs, :], lookup(below[qs], near, index))
                pick_s[i, g, qs, :] = jnp.where(over2, lookup(above[qs], near, index), pick)
            rep = rep_s.at[(i % 2) * 6 + 3 + g]
            rep[...] = pick_s[i, g, :, :64].T * cw[g]
            ag = jnp.zeros((PTS, 128), F32)
            for c in range(4):
                ag = ag + rep[pl.ds(c, PTS, stride=4), :]
            lgs.append(att[g] * (ag - jnp.sum(att[g] * ag, axis=0, keepdims=True)))
        l0 = jnp.concatenate([lgs[0], lgs[2][:, :TAIL]], axis=1)
        l1 = jnp.concatenate([lgs[1], lgs[2][:, TAIL : 2 * TAIL]], axis=1)
        lg_s[i * 2 * PTS : (i + 1) * 2 * PTS, :] = jnp.concatenate([l0, l1], axis=0).astype(BF)

    scale = 1.0 / float(images * bands * CELLS) ** 0.5

    def weights(n, blocks):
        for c in range(2):
            at = 0
            for block in blocks:
                w_s[n][c, at : at + block.shape[0], :] = block[:, c * 128 : (c + 1) * 128]
                at += block.shape[0]

    def pair_weights(n, pairs):
        first, last = pairs[0] * 2 * HEAD, (pairs[-1] + 1) * 2 * HEAD
        gv = dot(vg_s[0, first:last, :], halo_s[0])
        gv = gv + dot(vg_s[1, first:last, :], x)
        gv = gv + dot(vg_s[2, first:last, :], halo_s[1])
        weights(n, [gv, dot(samp_s[first:last, :], og)])

    def swap(n):
        return remote(cs_s[n], cr_s[n], core_sem.at[n, 0], core_sem.at[n, 1], partner)

    def swap_send(n):
        cs_s[n][...] = w_s[n][1 - core].astype(BF)
        swap(n).start()

    def piece(n, t, where):
        q = peer(t)
        return remote(
            ps_s[n].at[q], pr_s[n].at[chip], ps_sem.at[n], pr_sem.at[n], {"band": 2 * q + core}
        )

    def plane_send(n):
        swap(n).wait()
        half = w_s[n][core] + cr_s[n][...].astype(F32)
        ps_s[n][...] = half.astype(BF).reshape(ps_s[n].shape)
        each(1, chips, lambda t: piece(n, t, None).start())
        pr_s[n][chip] = ps_s[n][chip]

    def bulk(n):
        some = pl.ds(0, 15)
        return remote(
            ps_s[n].at[some], pr_s[n].at[some], ps_sem.at[n], pr_sem.at[n], partner
        )

    def across(n, t):
        q = lax.rem(image + t, images)
        spot = yr_s[n].at[image]
        return remote(spot, spot, ys_sem.at[n], yr_sem.at[n], {"dp": q})

    def across_bulk(n):
        some = yr_s[n].at[pl.ds(0, 3)]
        return remote(some, some, ys_sem.at[n], yr_sem.at[n], partner)

    slot = core * 16 + chip

    def direct(n, t):
        q = lax.rem(band + t, bands)
        return remote(
            ps_s[n].at[lax.rem(q, 2) * 16 + lax.div(q, 2)],
            pr_s[n].at[slot],
            ps_sem.at[n],
            pr_sem.at[n],
            {"band": q},
        )

    def direct_bulk(n):
        some = pl.ds(0, 31)
        return remote(
            ps_s[n].at[some], pr_s[n].at[some], ps_sem.at[n], pr_sem.at[n], partner
        )

    def direct_send(n):
        ps_s[n][...] = w_s[n][...].astype(BF).reshape(ps_s[n].shape)
        each(1, bands, lambda t: direct(n, t).start())
        pr_s[n][slot] = ps_s[n][slot]

    def across_send(n):
        pieces = []
        if n < 2:
            bulk(n).wait_recv()
            pieces = [pr_s[n][q] for q in range(16)]
        else:
            direct_bulk(n).wait_recv()
            pieces = [pr_s[n][q] for q in range(32)]
        sums = [piece.astype(F32) for piece in pieces]
        while len(sums) > 1:
            sums = [a + b for a, b in zip(sums[::2], sums[1::2])]
        yr_s[n][image] = sums[0]
        each(1, images, lambda t: across(n, t).start())

    def share(n, t):
        q = peer(t)
        spot = ag_refs[n].at[core, chip]
        return remote(spot, spot, as_sem.at[n], ar_sem.at[n], {"band": 2 * q + core})

    def share_bulk(n):
        some = ag_refs[n].at[core, pl.ds(0, 15)]
        return remote(some, some, as_sem.at[n], ar_sem.at[n], partner)

    def share_all(n, t):
        spot = ag_refs[n].at[slot]
        where = {"band": lax.rem(band + t, bands)}
        return remote(spot, spot, as_sem.at[n], ar_sem.at[n], where)

    def share_all_bulk(n):
        some = ag_refs[n].at[pl.ds(0, 31)]
        return remote(some, some, as_sem.at[n], ar_sem.at[n], partner)

    def share_send(n):
        across_bulk(n).wait_recv()
        total = yr_s[n][0]
        for q in range(1, images):
            total = total + yr_s[n][q]
        total = (total * scale).astype(BF)
        if n < 2:
            ag_refs[n][core, chip] = total
            each(1, chips, lambda t: share(n, t).start())
        else:
            ag_refs[n][slot] = total
            each(1, bands, lambda t: share_all(n, t).start())

    def relay(n, side):
        spot = ag_refs[n].at[side]
        return remote(spot, spot, rs_sem.at[n], rr_sem.at[n], partner)

    def relay_send(n):
        share_bulk(n).wait_recv()
        relay(n, core).start()

    def settle(n):
        across_bulk(n).wait_send()
        if n < 2:
            bulk(n).wait_send()
            share_bulk(n).wait_send()
            relay(n, core).wait_send()
        else:
            direct_bulk(n).wait_send()
            share_all_bulk(n).wait_send()

    def widen(v):
        return jnp.concatenate([v, jnp.zeros((D, D - CELLS), F32)], axis=1).astype(BF)

    def own(i):
        spread_grad(i)
        project_own(i)
        attend_own(i, built[i])

    built = [build(0)]
    for load in loads[4:]:
        load.wait()
    vwt_s[...] = vw_s[...].T
    og = og_s[...]
    g_s[...] = dot(ow_s[...], og, 1, 1).astype(BF).astype(F32)
    v_s[1] = widen(dot(vwt_s[...], x, 1, 1))
    for i in range(PAIRS):
        pick_s[i, 2, 2 * TAIL :, :] = jnp.zeros((128 - 2 * TAIL, 128), F32)
    built.append(build(1))
    own(0)

    pl.semaphore_wait(barrier, bands - 1 + images - 1)
    halo_up = remote(x_s, halo_s.at[0], halo_sem.at[0], halo_sem.at[2], up)
    halo_down = remote(x_s, halo_s.at[1], halo_sem.at[1], halo_sem.at[3], down)
    halo_up.start()
    halo_down.start()

    built.append(build(2))
    own(1)
    built.append(build(3))
    own(2)
    own(3)

    halo_up.wait()
    halo_down.wait()

    v_s[0] = widen(dot(vwt_s[...], halo_s[0], 1, 1))
    v_s[2] = widen(dot(vwt_s[...], halo_s[1], 1, 1))
    project_beside(0)
    project_beside(1)
    pair_weights(0, (0, 1))
    swap_send(0)
    project_beside(2)
    project_beside(3)
    pair_weights(1, (2, 3))
    swap_send(1)
    attend_beside(0, built[0])
    plane_send(0)
    plane_send(1)
    attend_beside(1, built[1])
    attend_beside(2, built[2])
    attend_beside(3, built[3])
    weights(2, [dot(lg_s[...], x)])
    direct_send(2)
    send_s[0] = vg_s[0].T
    send_s[1] = vg_s[2].T
    back_down = remote(send_s.at[0], back_s.at[1], back_sem.at[0], back_sem.at[2], down)
    back_up = remote(send_s.at[1], back_s.at[0], back_sem.at[1], back_sem.at[3], up)
    back_down.start()
    back_up.start()
    partial_grad = dot(lg_s[...].astype(F32).T.astype(BF), lw_s[...], 1, 1)
    own_t = own_s[...].T
    across_send(0)
    across_send(1)
    back_down.wait()
    back_up.wait()
    value_grad = own_t + back_s[0].astype(F32) + back_s[1].astype(F32)
    input_grad = dot(value_grad.astype(BF), vwt_s[...]) + partial_grad
    ig_ref[...] = input_grad.astype(BF)
    across_send(2)
    share_send(0)
    share_send(1)
    share_send(2)
    relay_send(0)
    relay_send(1)
    for n in range(2):
        relay(n, 1 - core).wait_recv()
    share_all_bulk(2).wait_recv()
    for n in range(3):
        settle(n)


def finish_kernel(aga_ref, agb_ref, agc_ref, ig_in, ig_ref, gv_ref, gl_ref, go_ref):
    ig_ref[...] = ig_in[...]
    for c in range(2):
        cols = slice(c * 128, (c + 1) * 128)
        a = aga_ref[c].reshape(CHUNKS[0], 128).astype(F32)
        b = agb_ref[c].reshape(CHUNKS[1], 128).astype(F32)
        gv_ref[cols, :128] = a[:128].T
        gv_ref[cols, 128:] = b[:128].T
        go_ref[:128, cols] = a[128:]
        go_ref[128:, cols] = b[128:]
        gl_ref[cols, :] = agc_ref[c * 16 : c * 16 + 16].reshape(CHUNKS[2], 128).astype(F32).T


def body(features, corner_rows, corner_weights, out_grad, vw, lw, ow):
    vm = pl.BlockSpec(memory_space=pltpu.VMEM)
    hbm = pl.BlockSpec(memory_space=pltpu.HBM)
    dma = pltpu.SemaphoreType.DMA
    ig, aga, agb, agc = pl.pallas_call(
        whole_kernel,
        out_shape=(
            pltpu.VMEM((CELLS, D), BF),
            pltpu.VMEM((2, 16, CHUNKS[0] // 16, 128), BF),
            pltpu.VMEM((2, 16, CHUNKS[1] // 16, 128), BF),
            pltpu.VMEM((32, CHUNKS[2] // 16, 128), BF),
        ),
        in_specs=[hbm] * 7,
        out_specs=[vm] * 4,
        scratch_shapes=[
            pltpu.VMEM((CELLS, D), BF),
            pltpu.VMEM((CELLS, D), BF),
            pltpu.VMEM((D, D), BF),
            pltpu.VMEM((D, HEADS * PTS), BF),
            pltpu.VMEM((D, D), BF),
            pltpu.VMEM((HEADS, 64, CELLS), I32),
            pltpu.VMEM((HEADS, 64, CELLS), F32),
            pltpu.VMEM((D, D), BF),
            pltpu.VMEM((2, CELLS, D), BF),
            pltpu.VMEM((3, D, D), BF),
            pltpu.VMEM((HEADS, PTS, CELLS), F32),
            pltpu.VMEM((D, CELLS), F32),
            pltpu.VMEM((D, CELLS), BF),
            pltpu.VMEM((12, 64, 128), F32),
            pltpu.VMEM((D, CELLS), F32),
            pltpu.VMEM((3, D, CELLS), BF),
            pltpu.VMEM((2, 3, 4, 64, 128), F32),
            pltpu.VMEM((PAIRS, 3, PAD, LANES), BF),
            pltpu.VMEM((HEADS * PTS, CELLS), BF),
            pltpu.VMEM((2, CELLS, D), BF),
            pltpu.VMEM((2, CELLS, D), BF),
            pltpu.VMEM((PAIRS, 2 * HEAD, LANES), BF),
            pltpu.VMEM((PAIRS, 3, 128, 2 * HEAD), BF),
            pltpu.VMEM((PAIRS, 2 * HEAD, LANES), F32),
            pltpu.VMEM((PAIRS, 3, 128, 128), I32),
            pltpu.VMEM((PAIRS, 3, 128, 128), F32),
            [pltpu.VMEM((2, n, 128), F32) for n in CHUNKS],
            [pltpu.VMEM((n, 128), BF) for n in CHUNKS[:2]],
            [pltpu.VMEM((n, 128), BF) for n in CHUNKS[:2]],
            [pltpu.VMEM((16, n // 16, 128), BF) for n in CHUNKS[:2]]
            + [pltpu.VMEM((32, n // 16, 128), BF) for n in CHUNKS[2:]],
            [pltpu.VMEM((16, n // 16, 128), BF) for n in CHUNKS[:2]]
            + [pltpu.VMEM((32, n // 16, 128), BF) for n in CHUNKS[2:]],
            [pltpu.VMEM((4, n // 16, 128), F32) for n in CHUNKS],
            dma((9,)),
            dma((4,)),
            dma((4,)),
            dma((2, 2)),
            dma((3,)),
            dma((3,)),
            dma((3,)),
            dma((3,)),
            dma((3,)),
            dma((3,)),
            dma((2,)),
            dma((2,)),
        ],
        compiler_params=pltpu.CompilerParams(
            collective_id=0, has_side_effects=True, vmem_limit_bytes=60 * 10**6
        ),
        name="whole",
    )(
        features[0].T,
        corner_rows[0],
        corner_weights[0],
        out_grad[0].T,
        vw,
        lw,
        ow,
    )
    ig, gv, gl, go = pl.pallas_call(
        finish_kernel,
        out_shape=(
            jax.ShapeDtypeStruct((CELLS, D), BF),
            jax.ShapeDtypeStruct((D, D), F32),
            jax.ShapeDtypeStruct((D, HEADS * PTS), F32),
            jax.ShapeDtypeStruct((D, D), F32),
        ),
        in_specs=[vm] * 4,
        out_specs=[vm] * 4,
        compiler_params=pltpu.CompilerParams(vmem_limit_bytes=8 * 2**20),
        name="finish",
    )(aga, agb, agc, ig)
    return (ig.T[None], gv, gl, go)


def solution(mesh):
    placed = (
        P("dp", None, "band"),
        P("dp", None, None, "band"),
        P("dp", None, None, "band"),
        P("dp", None, "band"),
        P(),
        P(),
        P(),
    )
    return jax.shard_map(
        body,
        mesh=mesh,
        in_specs=placed,
        out_specs=(P("dp", None, "band"), P(), P(), P()),
        check_vma=False,
    )
```

time: 39.9 us -> 33.2 us (0.83)
  Pallas kernels: 39.1 us -> 32.4 us
    pallas_call x1, Pallas kernels: 38.2 us -> 31.5 us  [body(): pl.pallas_call(whole_kernel, out_shape=(pltpu.VMEM((CELLS, D), BF), pltpu...]
where the time goes in v4:
time: 33.2 us; the launch traced here: 33.1 us
  Pallas kernels  32.4 us (98%)
  between operations  0.64 us (2%)
    pallas_call x1, Pallas kernels, body(): pl.pallas_call(whole_kernel, out_shape=(pltpu.VMEM((CELLS, D), BF), pltpu...  31.5 us
    pallas_call x1, Pallas kernels, body(): pl.pallas_call(finish_kernel, out_shape=(jax.ShapeDtypeStruct((CELLS, D),...  0.92 us

profile of v4, /device:TPU:1, one launch (start us, length us, event | category | flops | bytes accessed | tf_op | source)
XLA Modules:
  0.0 33.1 jit_solution(10009795417405189073)
XLA Ops:
  0.6 31.5 %whole.1 = (bf16[172,256]{1,0:T(8,128)(2,1)S(1)}, bf16[2,16,16,128]{3,2,1,0:T(8,128)(2,1)S(1)}, bf16[2,16,16,128]{3,2,1,0:T(8,128)(2,1)S(1)}, bf16[32,8,128]{2,1,0:T(8,128)(2,1)S(1)}) custom-call(bf16[172,256]{1,0:T(8,128)(2,1)} %bitcast.13, s32[8,64,172]{2,1,0:T(8,128)} %bitcast.11, f32[8,64,172]{2,1,0:T(8,128)} %bitcast.12, bf16[172,256]{1,0:T(8,128)(2,1)} %bitcast.14, ...), custom_call_target="tpu_custom_call" | custom-call | tf_op jit(solution)/shard_map/whole/pallas_call | solution.py:543
  32.1 0.9 %finish.1 = (bf16[172,256]{1,0:T(8,128)(2,1)}, f32[256,256]{1,0:T(8,128)}, f32[256,128]{1,0:T(8,128)}, f32[256,256]{1,0:T(8,128)}) custom-call(bf16[2,16,16,128]{3,2,1,0:T(8,128)(2,1)S(1)} %get-tuple-element.12.aga_ref, bf16[2,16,16,128]{3,2,1,0:T(8,128)(2,1)S(1)} %get-tuple-element.13.agb_ref, bf16[32,8,128]{2,1,0:T(8,128)(2,1)S(1)} %get-tuple-element.14.agc_ref, ...), custom_call_target="tpu_custom_call" | custom-call | tf_op jit(solution)/shard_map/finish/pallas_call | solution.py:614

commit v5 on v4

--- a/solution.py
+++ b/solution.py
@@ -15,6 +15,7 @@
 GAP = 128 - 2 * TAIL
 LANES = 384
 PAIRS = HEADS // 2
+SIDE = 4
 HEAD = D // HEADS
 PTS = LEVELS * POINTS
 CHUNKS = (256, 256, 128)
@@ -82,6 +83,7 @@
     half_s,
     at_s,
     pick_s,
+    rest_s,
     w_s,
     cs_s,
     cr_s,
@@ -113,8 +115,19 @@
     down = {"band": lax.rem(band + bands - 1, bands)}
     partner = {"band": band + 1 - 2 * core}
 
+    row, column = lax.div(chip, SIDE), lax.rem(chip, SIDE)
+    steps = [(a, b) for a in range(SIDE) for b in range(SIDE)]
+    steps.sort(key=lambda ab: -sum(min(n, SIDE - n) for n in ab))
+
     def peer(t):
-        return lax.rem(chip + t, chips)
+        a, b = steps[t - 1]
+        return lax.rem(row + a, SIDE) * SIDE + lax.rem(column + b, SIDE)
+
+    def side(t):
+        return core if t % 2 and t + 1 < bands else 1 - core
+
+    def any_peer(t):
+        return 2 * peer((t + 1) // 2) + side(t)
 
     def remote(src, dst, send, recv, where):
         return pltpu.make_async_remote_copy(
@@ -127,11 +140,8 @@
         )
 
     def each(low, high, step):
-        def run(t, carry):
+        for t in range(low, high):
             step(t)
-            return carry
-
-        lax.fori_loop(low, high, run, 0)
 
     barrier = pltpu.get_barrier_semaphore()
 
@@ -157,7 +167,7 @@
     ]
     for load in loads:
         load.start()
-    each(1, bands, lambda t: greet({"band": lax.rem(band + t, bands)}))
+    each(1, bands, lambda t: greet({"band": any_peer(t)}))
     each(1, images, lambda t: greet({"dp": lax.rem(image + t, images)}))
 
     loads[0].wait()
@@ -288,13 +298,17 @@
         _, cw, att = built
         lgs = []
         for g in range(3):
-            below = dot(gt_s[i, g], v_s[0, heads_of(i), :])
-            above = dot(gt_s[i, g], v_s[2, heads_of(i), :])
+            below = dot(gt_s[i, g], v_s[0, heads_of(i), :128])
+            above = dot(gt_s[i, g], v_s[2, heads_of(i), :128])
+            rest = dot(gt_s[i, g], rest_s[heads_of(i), :])
             for q in groups(g):
                 qs = slice(q, q + 8)
                 over1, over2, near, index = parts(at_s[i, g, qs, :])
-                pick = jnp.where(over1, pick_s[i, g, qs, :], lookup(below[qs], near, index))
-                pick_s[i, g, qs, :] = jnp.where(over2, lookup(above[qs], near, index), pick)
+                index = jnp.where(near, index, jnp.where(over2, index + TAIL, index))
+                pick = jnp.where(over2, lane_pick(above[qs], index), lane_pick(below[qs], index))
+                pick = jnp.where(near, pick, lane_pick(rest[qs], index))
+                mine = jnp.where(over2, pick, pick_s[i, g, qs, :])
+                pick_s[i, g, qs, :] = jnp.where(over1, mine, pick)
             rep = rep_s.at[(i % 2) * 6 + 3 + g]
             rep[...] = pick_s[i, g, :, :64].T * cw[g]
             ag = jnp.zeros((PTS, 128), F32)
@@ -359,9 +373,9 @@
     slot = core * 16 + chip
 
     def direct(n, t):
-        q = lax.rem(band + t, bands)
+        q = any_peer(t)
         return remote(
-            ps_s[n].at[lax.rem(q, 2) * 16 + lax.div(q, 2)],
+            ps_s[n].at[side(t) * 16 + peer((t + 1) // 2)],
             pr_s[n].at[slot],
             ps_sem.at[n],
             pr_sem.at[n],
@@ -404,7 +418,7 @@
 
     def share_all(n, t):
         spot = ag_refs[n].at[slot]
-        where = {"band": lax.rem(band + t, bands)}
+        where = {"band": any_peer(t)}
         return remote(spot, spot, as_sem.at[n], ar_sem.at[n], where)
 
     def share_all_bulk(n):
@@ -417,7 +431,7 @@
         for q in range(1, images):
             total = total + yr_s[n][q]
         total = (total * scale).astype(BF)
-        if n < 2:
+        if n < 1:
             ag_refs[n][core, chip] = total
             each(1, chips, lambda t: share(n, t).start())
         else:
@@ -434,12 +448,11 @@
 
     def settle(n):
         across_bulk(n).wait_send()
-        if n < 2:
-            bulk(n).wait_send()
+        (bulk if n < 2 else direct_bulk)(n).wait_send()
+        if n < 1:
             share_bulk(n).wait_send()
             relay(n, core).wait_send()
         else:
-            direct_bulk(n).wait_send()
             share_all_bulk(n).wait_send()
 
     def widen(v):
@@ -477,8 +490,13 @@
     halo_up.wait()
     halo_down.wait()
 
-    v_s[0] = widen(dot(vwt_s[...], halo_s[0], 1, 1))
-    v_s[2] = widen(dot(vwt_s[...], halo_s[1], 1, 1))
+    low = dot(vwt_s[...], halo_s[0], 1, 1)
+    high = dot(vwt_s[...], halo_s[1], 1, 1)
+    v_s[0] = widen(low)
+    v_s[2] = widen(high)
+    rest_s[...] = jnp.concatenate(
+        [low[:, 128:], high[:, 128:], jnp.zeros((D, GAP), F32)], axis=1
+    ).astype(BF)
     project_beside(0)
     project_beside(1)
     pair_weights(0, (0, 1))
@@ -488,9 +506,9 @@
     pair_weights(1, (2, 3))
     swap_send(1)
     attend_beside(0, built[0])
+    attend_beside(1, built[1])
     plane_send(0)
     plane_send(1)
-    attend_beside(1, built[1])
     attend_beside(2, built[2])
     attend_beside(3, built[3])
     weights(2, [dot(lg_s[...], x)])
@@ -515,25 +533,52 @@
     share_send(1)
     share_send(2)
     relay_send(0)
-    relay_send(1)
-    for n in range(2):
-        relay(n, 1 - core).wait_recv()
+    share_all_bulk(1).wait_recv()
     share_all_bulk(2).wait_recv()
+    relay(0, 1 - core).wait_recv()
     for n in range(3):
         settle(n)
 
 
-def finish_kernel(aga_ref, agb_ref, agc_ref, ig_in, ig_ref, gv_ref, gl_ref, go_ref):
-    ig_ref[...] = ig_in[...]
+def finish_kernel(
+    aga_ref, agb_ref, agc_ref, ig_in, ig_hbm, gv_hbm, gl_hbm, go_hbm, gv_s, gl_s, go_s, sem
+):
+    copies = [
+        pltpu.make_async_copy(src, dst, sem.at[n])
+        for n, (src, dst) in enumerate(
+            [
+                (ig_in, ig_hbm),
+                (go_s, go_hbm),
+                (gv_s.at[:128], gv_hbm.at[:128]),
+                (gv_s.at[128:], gv_hbm.at[128:]),
+                (gl_s, gl_hbm),
+            ]
+        )
+    ]
+    copies[0].start()
+    parts = [
+        (
+            aga_ref[c].reshape(CHUNKS[0], 128).astype(F32),
+            agb_ref[c * 16 : c * 16 + 16].reshape(CHUNKS[1], 128).astype(F32),
+        )
+        for c in range(2)
+    ]
+    for c, (a, b) in enumerate(parts):
+        cols = slice(c * 128, (c + 1) * 128)
+        go_s[:128, cols] = a[128:]
+        go_s[128:, cols] = b[128:]
+    copies[1].start()
+    for c, (a, b) in enumerate(parts):
+        cols = slice(c * 128, (c + 1) * 128)
+        gv_s[cols, :128] = a[:128].T
+        gv_s[cols, 128:] = b[:128].T
+        copies[2 + c].start()
     for c in range(2):
         cols = slice(c * 128, (c + 1) * 128)
-        a = aga_ref[c].reshape(CHUNKS[0], 128).astype(F32)
-        b = agb_ref[c].reshape(CHUNKS[1], 128).astype(F32)
-        gv_ref[cols, :128] = a[:128].T
-        gv_ref[cols, 128:] = b[:128].T
-        go_ref[:128, cols] = a[128:]
-        go_ref[128:, cols] = b[128:]
-        gl_ref[cols, :] = agc_ref[c * 16 : c * 16 + 16].reshape(CHUNKS[2], 128).astype(F32).T
+        gl_s[cols, :] = agc_ref[c * 16 : c * 16 + 16].reshape(CHUNKS[2], 128).astype(F32).T
+    copies[4].start()
+    for copy in copies:
+        copy.wait()
 
 
 def body(features, corner_rows, corner_weights, out_grad, vw, lw, ow):
@@ -545,7 +590,7 @@
         out_shape=(
             pltpu.VMEM((CELLS, D), BF),
             pltpu.VMEM((2, 16, CHUNKS[0] // 16, 128), BF),
-            pltpu.VMEM((2, 16, CHUNKS[1] // 16, 128), BF),
+            pltpu.VMEM((32, CHUNKS[1] // 16, 128), BF),
             pltpu.VMEM((32, CHUNKS[2] // 16, 128), BF),
         ),
         in_specs=[hbm] * 7,
@@ -577,6 +622,7 @@
             pltpu.VMEM((PAIRS, 2 * HEAD, LANES), F32),
             pltpu.VMEM((PAIRS, 3, 128, 128), I32),
             pltpu.VMEM((PAIRS, 3, 128, 128), F32),
+            pltpu.VMEM((D, 128), BF),
             [pltpu.VMEM((2, n, 128), F32) for n in CHUNKS],
             [pltpu.VMEM((n, 128), BF) for n in CHUNKS[:2]],
             [pltpu.VMEM((n, 128), BF) for n in CHUNKS[:2]],
@@ -595,8 +641,8 @@
             dma((3,)),
             dma((3,)),
             dma((3,)),
-            dma((2,)),
-            dma((2,)),
+            dma((1,)),
+            dma((1,)),
         ],
         compiler_params=pltpu.CompilerParams(
             collective_id=0, has_side_effects=True, vmem_limit_bytes=60 * 10**6
@@ -620,7 +666,13 @@
             jax.ShapeDtypeStruct((D, D), F32),
         ),
         in_specs=[vm] * 4,
-        out_specs=[vm] * 4,
+        out_specs=[hbm] * 4,
+        scratch_shapes=[
+            pltpu.VMEM((D, D), F32),
+            pltpu.VMEM((D, HEADS * PTS), F32),
+            pltpu.VMEM((D, D), F32),
+            dma((5,)),
+        ],
         compiler_params=pltpu.CompilerParams(vmem_limit_bytes=8 * 2**20),
         name="finish",
     )(aga, agb, agc, ig)

time: 33.2 us -> 32.2 us (0.970)
  Pallas kernels: 32.4 us -> 31.5 us
    pallas_call x1, Pallas kernels: 31.5 us -> 30.6 us  [body(): pl.pallas_call(whole_kernel, out_shape=(pltpu.VMEM((CELLS, D), BF), pltpu...]
where the time goes in v5:
time: 32.2 us; the launch traced here: 32.1 us
  Pallas kernels  31.5 us (98%)
  between operations  0.64 us (2%)
    pallas_call x1, Pallas kernels, body(): pl.pallas_call(whole_kernel, out_shape=(pltpu.VMEM((CELLS, D), BF), pltpu...  30.6 us
    pallas_call x1, Pallas kernels, body(): pl.pallas_call(finish_kernel, out_shape=(jax.ShapeDtypeStruct((CELLS, D),...  0.92 us

profile of v5, /device:TPU:1, one launch (start us, length us, event | category | flops | bytes accessed | tf_op | source)
XLA Modules:
  0.0 32.1 jit_solution(11242051375172581811)
XLA Ops:
  0.6 30.6 %whole.1 = (bf16[172,256]{1,0:T(8,128)(2,1)S(1)}, bf16[2,16,16,128]{3,2,1,0:T(8,128)(2,1)S(1)}, bf16[32,16,128]{2,1,0:T(8,128)(2,1)S(1)}, bf16[32,8,128]{2,1,0:T(8,128)(2,1)S(1)}) custom-call(bf16[172,256]{1,0:T(8,128)(2,1)} %bitcast.13, s32[8,64,172]{2,1,0:T(8,128)} %bitcast.11, f32[8,64,172]{2,1,0:T(8,128)} %bitcast.12, bf16[172,256]{1,0:T(8,128)(2,1)} %bitcast.14, ...), custom_call_target="tpu_custom_call" | custom-call | tf_op jit(solution)/shard_map/whole/pallas_call | solution.py:588
  31.2 0.9 %finish.1 = (bf16[172,256]{1,0:T(8,128)(2,1)}, f32[256,256]{1,0:T(8,128)}, f32[256,128]{1,0:T(8,128)}, f32[256,256]{1,0:T(8,128)}) custom-call(bf16[2,16,16,128]{3,2,1,0:T(8,128)(2,1)S(1)} %get-tuple-element.12.aga_ref, bf16[32,16,128]{2,1,0:T(8,128)(2,1)S(1)} %get-tuple-element.13.agb_ref, bf16[32,8,128]{2,1,0:T(8,128)(2,1)S(1)} %get-tuple-element.14.agc_ref, ...), custom_call_target="tpu_custom_call" | custom-call | tf_op jit(solution)/shard_map/finish/pallas_call | solution.py:660

commit v6 on v5

--- a/solution.py
+++ b/solution.py
@@ -259,19 +259,18 @@
 
     def project_own(i):
         hs = heads_of(i)
-        m_j = m_s[i, 1, :CELLS, :]
-        half_s[i] = dot(v_s[1, hs, :CELLS], m_j)
-        part = dot(gp_s[i], m_j, 1, 1)
-        own_s[hs, :] = part
-        vg_s[1, hs, :] = part.astype(BF)
+        half_s[i] = dot(v_s[1, hs, :CELLS], m_s[i, 1, :CELLS, :])
+        for j in range(3):
+            part = dot(gp_s[i], m_s[i, j, :CELLS, :], 1, 1)
+            if j == 1:
+                own_s[hs, :] = part
+            vg_s[j, hs, :] = part.astype(BF)
 
     def project_beside(i):
         hs = heads_of(i)
         samp = half_s[i]
         for j in (0, 2):
-            m_j = m_s[i, j, :CELLS, :]
-            samp = samp + dot(v_s[j, hs, :CELLS], m_j)
-            vg_s[j, hs, :] = dot(gp_s[i], m_j, 1, 1).astype(BF)
+            samp = samp + dot(v_s[j, hs, :CELLS], m_s[i, j, :CELLS, :])
         s0 = jnp.concatenate([samp[:HEAD, :128], samp[:HEAD, 256 : 256 + TAIL]], axis=1)
         s1 = jnp.concatenate(
             [samp[HEAD:, 128:256], samp[HEAD:, 256 + TAIL : 256 + 2 * TAIL]], axis=1
@@ -395,7 +394,7 @@
 
     def across_send(n):
         pieces = []
-        if n < 2:
+        if n < 1:
             bulk(n).wait_recv()
             pieces = [pr_s[n][q] for q in range(16)]
         else:
@@ -405,7 +404,7 @@
         while len(sums) > 1:
             sums = [a + b for a, b in zip(sums[::2], sums[1::2])]
         yr_s[n][image] = sums[0]
-        each(1, images, lambda t: across(n, t).start())
+        each(0, images - 1, lambda t: across(n, (2, 1, 3)[t]).start())
 
     def share(n, t):
         q = peer(t)
@@ -448,7 +447,7 @@
 
     def settle(n):
         across_bulk(n).wait_send()
-        (bulk if n < 2 else direct_bulk)(n).wait_send()
+        (bulk if n < 1 else direct_bulk)(n).wait_send()
         if n < 1:
             share_bulk(n).wait_send()
             relay(n, core).wait_send()
@@ -487,6 +486,12 @@
     own(2)
     own(3)
 
+    send_s[0] = vg_s[0].T
+    send_s[1] = vg_s[2].T
+    back_down = remote(send_s.at[0], back_s.at[1], back_sem.at[0], back_sem.at[2], down)
+    back_up = remote(send_s.at[1], back_s.at[0], back_sem.at[1], back_sem.at[3], up)
+    back_down.start()
+    back_up.start()
     halo_up.wait()
     halo_down.wait()
 
@@ -497,28 +502,19 @@
     rest_s[...] = jnp.concatenate(
         [low[:, 128:], high[:, 128:], jnp.zeros((D, GAP), F32)], axis=1
     ).astype(BF)
-    project_beside(0)
-    project_beside(1)
+    for i in range(PAIRS):
+        project_beside(i)
     pair_weights(0, (0, 1))
+    pair_weights(1, (2, 3))
     swap_send(0)
-    project_beside(2)
-    project_beside(3)
-    pair_weights(1, (2, 3))
-    swap_send(1)
+    direct_send(1)
     attend_beside(0, built[0])
     attend_beside(1, built[1])
     plane_send(0)
-    plane_send(1)
     attend_beside(2, built[2])
     attend_beside(3, built[3])
     weights(2, [dot(lg_s[...], x)])
     direct_send(2)
-    send_s[0] = vg_s[0].T
-    send_s[1] = vg_s[2].T
-    back_down = remote(send_s.at[0], back_s.at[1], back_sem.at[0], back_sem.at[2], down)
-    back_up = remote(send_s.at[1], back_s.at[0], back_sem.at[1], back_sem.at[3], up)
-    back_down.start()
-    back_up.start()
     partial_grad = dot(lg_s[...].astype(F32).T.astype(BF), lw_s[...], 1, 1)
     own_t = own_s[...].T
     across_send(0)
@@ -624,17 +620,17 @@
             pltpu.VMEM((PAIRS, 3, 128, 128), F32),
             pltpu.VMEM((D, 128), BF),
             [pltpu.VMEM((2, n, 128), F32) for n in CHUNKS],
-            [pltpu.VMEM((n, 128), BF) for n in CHUNKS[:2]],
-            [pltpu.VMEM((n, 128), BF) for n in CHUNKS[:2]],
-            [pltpu.VMEM((16, n // 16, 128), BF) for n in CHUNKS[:2]]
-            + [pltpu.VMEM((32, n // 16, 128), BF) for n in CHUNKS[2:]],
-            [pltpu.VMEM((16, n // 16, 128), BF) for n in CHUNKS[:2]]
-            + [pltpu.VMEM((32, n // 16, 128), BF) for n in CHUNKS[2:]],
+            [pltpu.VMEM((n, 128), BF) for n in CHUNKS[:1]],
+            [pltpu.VMEM((n, 128), BF) for n in CHUNKS[:1]],
+            [pltpu.VMEM((16, n // 16, 128), BF) for n in CHUNKS[:1]]
+            + [pltpu.VMEM((32, n // 16, 128), BF) for n in CHUNKS[1:]],
+            [pltpu.VMEM((16, n // 16, 128), BF) for n in CHUNKS[:1]]
+            + [pltpu.VMEM((32, n // 16, 128), BF) for n in CHUNKS[1:]],
             [pltpu.VMEM((4, n // 16, 128), F32) for n in CHUNKS],
             dma((9,)),
             dma((4,)),
             dma((4,)),
-            dma((2, 2)),
+            dma((1, 2)),
             dma((3,)),
             dma((3,)),
             dma((3,)),

time: 32.2 us -> 31.7 us (0.984)
  Pallas kernels: 31.5 us -> 30.9 us
    pallas_call x1, Pallas kernels: 30.6 us -> 30 us  [body(): pl.pallas_call(whole_kernel, out_shape=(pltpu.VMEM((CELLS, D), BF), pltpu...]
where the time goes in v6:
time: 31.7 us; the launch traced here: 31.6 us
  Pallas kernels  30.9 us (97%)
  between operations  0.64 us (2%)
    pallas_call x1, Pallas kernels, body(): pl.pallas_call(whole_kernel, out_shape=(pltpu.VMEM((CELLS, D), BF), pltpu...  30 us
    pallas_call x1, Pallas kernels, body(): pl.pallas_call(finish_kernel, out_shape=(jax.ShapeDtypeStruct((CELLS, D),...  0.92 us

profile of v6, /device:TPU:1, one launch (start us, length us, event | category | flops | bytes accessed | tf_op | source)
XLA Modules:
  0.0 31.6 jit_solution(1709534697394374675)
XLA Ops:
  0.6 30.0 %whole.1 = (bf16[172,256]{1,0:T(8,128)(2,1)S(1)}, bf16[2,16,16,128]{3,2,1,0:T(8,128)(2,1)S(1)}, bf16[32,16,128]{2,1,0:T(8,128)(2,1)S(1)}, bf16[32,8,128]{2,1,0:T(8,128)(2,1)S(1)}) custom-call(bf16[172,256]{1,0:T(8,128)(2,1)} %bitcast.13, s32[8,64,172]{2,1,0:T(8,128)} %bitcast.11, f32[8,64,172]{2,1,0:T(8,128)} %bitcast.12, bf16[172,256]{1,0:T(8,128)(2,1)} %bitcast.14, ...), custom_call_target="tpu_custom_call" | custom-call | tf_op jit(solution)/shard_map/whole/pallas_call | solution.py:584
  30.7 0.9 %finish.1 = (bf16[172,256]{1,0:T(8,128)(2,1)}, f32[256,256]{1,0:T(8,128)}, f32[256,128]{1,0:T(8,128)}, f32[256,256]{1,0:T(8,128)}) custom-call(bf16[2,16,16,128]{3,2,1,0:T(8,128)(2,1)S(1)} %get-tuple-element.12.aga_ref, bf16[32,16,128]{2,1,0:T(8,128)(2,1)S(1)} %get-tuple-element.13.agb_ref, bf16[32,8,128]{2,1,0:T(8,128)(2,1)S(1)} %get-tuple-element.14.agc_ref, ...), custom_call_target="tpu_custom_call" | custom-call | tf_op jit(solution)/shard_map/finish/pallas_call | solution.py:656

commit v7 on v6

--- a/solution.py
+++ b/solution.py
@@ -85,15 +85,12 @@
     pick_s,
     rest_s,
     w_s,
-    cs_s,
-    cr_s,
     ps_s,
     pr_s,
     yr_s,
     in_sem,
     halo_sem,
     back_sem,
-    core_sem,
     ps_sem,
     pr_sem,
     ys_sem,
@@ -334,32 +331,6 @@
         gv = gv + dot(vg_s[2, first:last, :], halo_s[1])
         weights(n, [gv, dot(samp_s[first:last, :], og)])
 
-    def swap(n):
-        return remote(cs_s[n], cr_s[n], core_sem.at[n, 0], core_sem.at[n, 1], partner)
-
-    def swap_send(n):
-        cs_s[n][...] = w_s[n][1 - core].astype(BF)
-        swap(n).start()
-
-    def piece(n, t, where):
-        q = peer(t)
-        return remote(
-            ps_s[n].at[q], pr_s[n].at[chip], ps_sem.at[n], pr_sem.at[n], {"band": 2 * q + core}
-        )
-
-    def plane_send(n):
-        swap(n).wait()
-        half = w_s[n][core] + cr_s[n][...].astype(F32)
-        ps_s[n][...] = half.astype(BF).reshape(ps_s[n].shape)
-        each(1, chips, lambda t: piece(n, t, None).start())
-        pr_s[n][chip] = ps_s[n][chip]
-
-    def bulk(n):
-        some = pl.ds(0, 15)
-        return remote(
-            ps_s[n].at[some], pr_s[n].at[some], ps_sem.at[n], pr_sem.at[n], partner
-        )
-
     def across(n, t):
         q = lax.rem(image + t, images)
         spot = yr_s[n].at[image]
@@ -393,13 +364,8 @@
         pr_s[n][slot] = ps_s[n][slot]
 
     def across_send(n):
-        pieces = []
-        if n < 1:
-            bulk(n).wait_recv()
-            pieces = [pr_s[n][q] for q in range(16)]
-        else:
-            direct_bulk(n).wait_recv()
-            pieces = [pr_s[n][q] for q in range(32)]
+        direct_bulk(n).wait_recv()
+        pieces = [pr_s[n][q] for q in range(32)]
         sums = [piece.astype(F32) for piece in pieces]
         while len(sums) > 1:
             sums = [a + b for a, b in zip(sums[::2], sums[1::2])]
@@ -447,7 +413,7 @@
 
     def settle(n):
         across_bulk(n).wait_send()
-        (bulk if n < 1 else direct_bulk)(n).wait_send()
+        direct_bulk(n).wait_send()
         if n < 1:
             share_bulk(n).wait_send()
             relay(n, core).wait_send()
@@ -505,12 +471,11 @@
     for i in range(PAIRS):
         project_beside(i)
     pair_weights(0, (0, 1))
+    direct_send(0)
     pair_weights(1, (2, 3))
-    swap_send(0)
     direct_send(1)
     attend_beside(0, built[0])
     attend_beside(1, built[1])
-    plane_send(0)
     attend_beside(2, built[2])
     attend_beside(3, built[3])
     weights(2, [dot(lg_s[...], x)])
@@ -620,17 +585,12 @@
             pltpu.VMEM((PAIRS, 3, 128, 128), F32),
             pltpu.VMEM((D, 128), BF),
             [pltpu.VMEM((2, n, 128), F32) for n in CHUNKS],
-            [pltpu.VMEM((n, 128), BF) for n in CHUNKS[:1]],
-            [pltpu.VMEM((n, 128), BF) for n in CHUNKS[:1]],
-            [pltpu.VMEM((16, n // 16, 128), BF) for n in CHUNKS[:1]]
-            + [pltpu.VMEM((32, n // 16, 128), BF) for n in CHUNKS[1:]],
-            [pltpu.VMEM((16, n // 16, 128), BF) for n in CHUNKS[:1]]
-            + [pltpu.VMEM((32, n // 16, 128), BF) for n in CHUNKS[1:]],
+            [pltpu.VMEM((32, n // 16, 128), BF) for n in CHUNKS],
+            [pltpu.VMEM((32, n // 16, 128), BF) for n in CHUNKS],
             [pltpu.VMEM((4, n // 16, 128), F32) for n in CHUNKS],
             dma((9,)),
             dma((4,)),
             dma((4,)),
-            dma((1, 2)),
             dma((3,)),
             dma((3,)),
             dma((3,)),

time: 31.7 us -> 31.6 us (level)
  no operation moved by 1% of the time
where the time goes in v7:
time: 31.6 us; the launch traced here: 31.5 us
  Pallas kernels  30.8 us (97%)
  between operations  0.64 us (2%)
    pallas_call x1, Pallas kernels, body(): pl.pallas_call(whole_kernel, out_shape=(pltpu.VMEM((CELLS, D), BF), pltpu...  29.9 us
    pallas_call x1, Pallas kernels, body(): pl.pallas_call(finish_kernel, out_shape=(jax.ShapeDtypeStruct((CELLS, D),...  0.92 us

profile of v7, /device:TPU:1, one launch (start us, length us, event | category | flops | bytes accessed | tf_op | source)
XLA Modules:
  0.0 31.5 jit_solution(6294347133812951756)
XLA Ops:
  0.6 29.9 %whole.1 = (bf16[172,256]{1,0:T(8,128)(2,1)S(1)}, bf16[2,16,16,128]{3,2,1,0:T(8,128)(2,1)S(1)}, bf16[32,16,128]{2,1,0:T(8,128)(2,1)S(1)}, bf16[32,8,128]{2,1,0:T(8,128)(2,1)S(1)}) custom-call(bf16[172,256]{1,0:T(8,128)(2,1)} %bitcast.13, s32[8,64,172]{2,1,0:T(8,128)} %bitcast.11, f32[8,64,172]{2,1,0:T(8,128)} %bitcast.12, bf16[172,256]{1,0:T(8,128)(2,1)} %bitcast.14, ...), custom_call_target="tpu_custom_call" | custom-call | tf_op jit(solution)/shard_map/whole/pallas_call | solution.py:549
  30.5 0.9 %finish.1 = (bf16[172,256]{1,0:T(8,128)(2,1)}, f32[256,256]{1,0:T(8,128)}, f32[256,128]{1,0:T(8,128)}, f32[256,256]{1,0:T(8,128)}) custom-call(bf16[2,16,16,128]{3,2,1,0:T(8,128)(2,1)S(1)} %get-tuple-element.12.aga_ref, bf16[32,16,128]{2,1,0:T(8,128)(2,1)S(1)} %get-tuple-element.13.agb_ref, bf16[32,8,128]{2,1,0:T(8,128)(2,1)S(1)} %get-tuple-element.14.agc_ref, ...), custom_call_target="tpu_custom_call" | custom-call | tf_op jit(solution)/shard_map/finish/pallas_call | solution.py:616
